TPU v7x, 32 devices: a whole 2x2x4 slice. The times are simulated.
32 devices in a mesh: grp: 2 (over x), node: 8 (over z, y), tm: 2 (over core).
Axes of the slice: x: 2, y: 2, z: 4, core: 2. Of those that a mesh axis runs over, the one named last changes fastest.
Arguments:
- scaled_kelvin: float32 [128, 8192], P(('grp', 'node', 'tm')), parts along dimension 0, may hold values from 0.5 to 1.5
- surface_emittance: float32 [16384], P('grp'), parts along dimension 0, may hold values from 0.2 to 1
- loss_factors: float32 [128, 8192], P(('grp', 'node', 'tm')), parts along dimension 0, may hold values from -6 to 6
- gebhart_tiles: bfloat16 [128, 32, 128, 128], P(('grp', 'node')), parts along dimension 0, may hold values from 1.4603138e-06 to 0.0014648438
- tile_target_index: int32 [128, 32], P(('grp', 'node')), parts along dimension 0, may hold values from 0 to 63
- tile_slots_occupied: int32 [128], P(('grp', 'node')), parts along dimension 0, may hold values from 16 to 32, as said below
Outputs:
- temp_sensitivity: float32 [128, 8192], P(('grp', 'node', 'tm')), parts along dimension 0
There are 2 independent parts, one for each index of `grp`. A program takes and returns all parts, laid end to end along the dimension named above; each array names one. Nothing has to cross between parts.
Inputs may be any that keep to these rules, and one draw needn't show every extreme that they name: A row's slots k below tile_slots_occupied are used, the others are ignored; some row of every variant uses all 32.
All inputs are finite; a program needn't handle non-finite values.
Results may differ from a plain program's by a relative error of at most 0.0036.
Values may be sent and summed in bfloat16 or wider, within the bound.
No kernel may reach another device: no remote copies, remote signals or barrier semaphores. Data moves between devices by JAX's collectives and lax.ppermute only.
A program may use at most 192 MiB of HBM per device.

v0:
```python
import jax
import jax.numpy as jnp
from jax import lax
from jax.sharding import PartitionSpec as P


def slot_window(gebhart_tiles, tile_target_index, tile_slots_occupied, slot_start, slot_width):
    in_use = (slot_start + jnp.arange(slot_width, dtype=jnp.int32))[None, :] < tile_slots_occupied[
        :, None
    ]
    return (gebhart_tiles, tile_target_index, in_use)


def over_slots(update, initial, slot_total):
    return update(initial, 0, slot_total)


def on_device(
    scaled_kelvin,
    surface_emittance,
    loss_factors,
    gebhart_tiles,
    tile_target_index,
    tile_slots_occupied,
):
    row_blocks, slot_total, block_side = (
        gebhart_tiles.shape[0],
        gebhart_tiles.shape[1],
        gebhart_tiles.shape[2],
    )
    surface_range = scaled_kelvin.shape[1]
    blocks_all = surface_range // block_side
    own_width = row_blocks * block_side
    own_start = lax.axis_index("node") * own_width
    radiant_output = (surface_emittance[None, :] * scaled_kelvin**4).astype(jnp.bfloat16)
    weights_here = lax.all_to_all(loss_factors, "node", split_axis=1, concat_axis=0, tiled=True)
    panel_rows = lax.all_gather(radiant_output, "node", axis=0, tiled=True)
    row_count = panel_rows.shape[0]
    panel_view = panel_rows.reshape(row_count, blocks_all, block_side)

    def update(running, slot_start, slot_width):
        tiles, columns, in_use = slot_window(
            gebhart_tiles, tile_target_index, tile_slots_occupied, slot_start, slot_width
        )
        picked = jnp.take(panel_view, columns.reshape(-1), axis=1)
        picked = picked.reshape(row_count, row_blocks, slot_width, block_side)
        picked = picked * in_use[None, :, :, None].astype(jnp.bfloat16)
        return jnp.einsum("nrkj,rkij->rni", picked, tiles, preferred_element_type=jnp.float32)

    flux = over_slots(
        update, jnp.zeros((row_blocks, row_count, block_side), jnp.float32), slot_total
    )
    flux = flux.transpose(1, 0, 2).reshape(row_count, own_width)
    own_emit = lax.dynamic_slice_in_dim(panel_rows, own_start, own_width, 1).astype(jnp.float32)
    weight_part = weights_here
    weight = weight_part * (flux - own_emit)
    sample_total = weight.shape[0]
    weight_rows = (
        weight.astype(jnp.bfloat16).reshape(sample_total, row_blocks, block_side).transpose(1, 0, 2)
    )
    weight_part = weight_rows

    def update(running, slot_start, slot_width):
        tiles, columns, in_use = slot_window(
            gebhart_tiles, tile_target_index, tile_slots_occupied, slot_start, slot_width
        )
        contrib = jnp.einsum(
            "rni,rkij->nrkj", weight_part, tiles, preferred_element_type=jnp.float32
        )
        targets = jnp.where(in_use, columns, blocks_all).reshape(-1)
        contrib = contrib.reshape(sample_total, row_blocks * slot_width, block_side)
        return running.at[:, targets, :].add(contrib, mode="drop")

    collected = over_slots(
        update, jnp.zeros((sample_total, blocks_all, block_side), jnp.float32), slot_total
    )
    summed = (
        lax.psum_scatter(
            collected.reshape(sample_total, surface_range).astype(jnp.bfloat16),
            "node",
            scatter_dimension=1,
            tiled=True,
        ).astype(jnp.float32)
        - weight
    )
    costate_vector = lax.all_to_all(summed, "node", split_axis=0, concat_axis=1, tiled=True)
    return 4.0 * surface_emittance[None, :] * scaled_kelvin**3 * costate_vector


def solution(mesh):
    placed = (
        P(("grp", "node", "tm"), None),
        P("grp"),
        P(("grp", "node", "tm"), None),
        P(("grp", "node"), None, None, None),
        P(("grp", "node"), None),
        P(("grp", "node")),
    )
    return jax.shard_map(
        on_device,
        mesh=mesh,
        in_specs=placed,
        out_specs=P(("grp", "node", "tm"), None),
        check_vma=False,
    )
```

profile of v0, /device:TPU:0, one launch (start us, length us, event | category | flops | bytes accessed | tf_op | source)
XLA Modules:
  0.0 169.4 jit_solution(2546197744501569730)
XLA Ops:
  6.5 7.3 %all-to-all-start = ((f32[4,8,1024]{2,0,1:T(4,128)}), f32[4,8,1024]{2,0,1:T(4,128)S(1)}, u32[]{:S(2)}, u32[]{:S(2)}) async-start(f32[4,8,1024]{2,0,1:T(4,128)} %bitcast.50), calls=%async_computation | async-start | bytes 262144 | tf_op jit(solution)/shard_map/all_to_all | solution.py:36
  13.8 0.0 reduce-scatter.2.cloned.1.call-start
  13.9 0.9 fusion.14
  14.8 31.9 %all-gather = bf16[8,4,8192]{2,1,0:T(4,128)(2,1)S(1)} all-gather(bf16[1,4,8192]{2,1,0:T(4,128)(2,1)S(1)} %fusion.14), channel_id=1, replica_groups=mesh['grp'=2,'node'=8,'tm'=2] {'node'}, dimensions={0}, use_global_device_ids=true | all-gather | bytes 589824 | tf_op jit(solution)/shard_map/all_gather | solution.py:37
  46.7 0.5 reshape.117
  47.3 0.3 copy.19
  47.6 0.8 reshape.118
  48.4 0.8 fusion.17
  49.2 1.0 gather_fusion
  50.2 5.2 %fusion.4 = f32[8,4,8,128]{3,2,1,0:T(8,128)S(1)} fusion(bf16[8,32,128,128]{3,2,1,0:T(8,128)(2,1)} %param.9, bf16[32,8,32,128]{3,0,2,1:T(8,128)(2,1)S(1)} %bitcast.46, pred[8,32]{1,0:T(8,128)(4,1)S(1)} %get-tuple-element.6, bf16[8,32]{1,0:T(8,128)(2,1)S(1)} %get-tuple-element.5), kind=kOutput, calls=%fused_computation.6 | convolution fusion | flops 270532608 | bytes 10617600 | tf_op jit(solution)/shard_map/nrkj,rkij->rni/dot_general | solution.py:48
  55.4 0.1 fusion.18
  55.5 0.1 reshape.139
  55.6 0.1 reshape.116
  55.8 6.6 %fusion.15 = f32[8,32,32,128]{3,1,2,0:T(8,128)} fusion(bf16[8,32,128,128]{3,2,1,0:T(8,128)(2,1)} %param.9, bf16[8,32,128,1]{2,0,1,3:T(8,128)(2,1)S(1)} %bitcast.49), kind=kOutput, calls=%fused_computation.21 | convolution fusion | flops 268435456 | bytes 12648448 | tf_op jit(solution)/shard_map/rni,rkij->nrkj/dot_general | solution.py:67
  62.4 0.1 broadcast_in_dim.16
  62.5 22.6 %scatter_fusion = f32[32,64,128]{2,0,1:T(8,128)S(1)} fusion(f32[32,64,128]{2,0,1:T(8,128)S(1)} %broadcast_in_dim.16, s32[256]{0:T(256)S(1)} %bitcast.51, f32[256,32,128]{2,1,0:T(8,128)} %bitcast.45), kind=kCustom, calls=%fused_computation.1 | custom fusion | flops 1048576 | bytes 12583936 | tf_op jit(solution)/shard_map/scatter-add | solution.py:72
  85.1 0.8 copy_bitcast_fusion
  86.0 0.0 reduce-scatter.2.cloned.1.call-update
  86.0 63.4 %reduce-scatter.2.cloned.1.call-done = bf16[32,1024]{1,0:T(8,128)(2,1)} async-done(((bf16[32,8192]{1,0:T(8,128)(2,1)}), bf16[32,1024]{1,0:T(8,128)(2,1)}) %reduce-scatter.2.cloned.1.call-update) | async-done | bytes 65552 | tf_op jit(solution)/shard_map/reduce_scatter | solution.py:78
  149.3 0.9 convert_subtract_fusion
  150.2 0.7 all_to_all.32
  150.9 3.6 %all-to-all-start.1 = ((f32[8,4,1024]{2,1,0:T(4,128)}), f32[8,4,1024]{2,1,0:T(4,128)S(1)}, u32[]{:S(2)}, u32[]{:S(2)}) async-start(f32[8,4,1024]{2,1,0:T(4,128)} %all_to_all.32), calls=%async_computation.2 | async-start | bytes 262144 | tf_op jit(solution)/shard_map/all_to_all | solution.py:86
  154.5 7.3 %all-to-all-done.1 = f32[8,4,1024]{2,1,0:T(4,128)S(1)} async-done(((f32[8,4,1024]{2,1,0:T(4,128)}), f32[8,4,1024]{2,1,0:T(4,128)S(1)}, u32[]{:S(2)}, u32[]{:S(2)}) %all-to-all-start.1) | async-done | bytes 131104 | tf_op jit(solution)/shard_map/all_to_all | solution.py:86
  161.9 0.7 fusion.10
  (16 shorter events, 0.2 us)
Async XLA Ops:
  6.5 49.2 %all-to-all-start = ((f32[4,8,1024]{2,0,1:T(4,128)}), f32[4,8,1024]{2,0,1:T(4,128)S(1)}, u32[]{:S(2)}, u32[]{:S(2)}) async-start(f32[4,8,1024]{2,0,1:T(4,128)} %bitcast.50), calls=%async_computation | async-start | bytes 262144 | tf_op jit(solution)/shard_map/all_to_all | solution.py:36
  13.8 135.5 %reduce-scatter.2.cloned.1.call-start = ((), (), s32[]{:S(2)}) async-start(), calls=%async_computation.3 | async-start | bytes 589824 | tf_op jit(solution)/shard_map/reduce_scatter | solution.py:78
  50.2 5.2 %copy-start.2 = (s32[8,32]{1,0:T(8,128)S(1)}, s32[8,32]{1,0:T(8,128)}, u32[]{:S(2)}) copy-start(s32[8,32]{1,0:T(8,128)} %param.10) | copy-start | bytes 3076
  50.2 5.2 %copy-start.3 = (s32[8]{0:T(128)S(1)}, s32[8]{0:T(128)}, u32[]{:S(2)}) copy-start(s32[8]{0:T(128)} %param.11) | copy-start | bytes 100
  62.5 92.0 %copy-start.1 = (f32[8192]{0:T(1024)S(1)}, f32[8192]{0:T(1024)}, u32[]{:S(2)}) copy-start(f32[8192]{0:T(1024)} %param.7) | copy-start | bytes 98308
  62.5 99.3 %copy-start = (f32[4,8192]{1,0:T(4,128)S(1)}, f32[4,8192]{1,0:T(4,128)}, u32[]{:S(2)}) copy-start(f32[4,8192]{1,0:T(4,128)} %param.6) | copy-start | bytes 393220
  150.9 11.0 %all-to-all-start.1 = ((f32[8,4,1024]{2,1,0:T(4,128)}), f32[8,4,1024]{2,1,0:T(4,128)S(1)}, u32[]{:S(2)}, u32[]{:S(2)}) async-start(f32[8,4,1024]{2,1,0:T(4,128)} %all_to_all.32), calls=%async_computation.2 | async-start | bytes 262144 | tf_op jit(solution)/shard_map/all_to_all | solution.py:86
Sparse Core Ops, SparseCore 0:
  86.1 63.1 reduce-scatter.1
where the time goes:
time: 170 us; the launch traced here: 169 us
  waiting for transfers between devices  70.7 us (42%)
  blocking collectives  31.9 us (19%)
  other arithmetic  26.8 us (16%)
  between operations  13.5 us (8%)
  matrix products  11.7 us (7%)
  starting transfers between devices  10.9 us (6%)
  local copies, waits for them, and re-layouts  3.74 us (2%)
    reduce_scatter x1, waiting for transfers between devices, on_device(): lax.psum_scatter(collected.reshape(sample_total, surface_range).astype(jn...  63.4 us
    all_gather x1, blocking collectives, on_device(): panel_rows = lax.all_gather(radiant_output, 'node', axis=0, tiled=True)  31.9 us
    scatter-add x1, other arithmetic, update(): return running.at[:, targets, :].add(contrib, mode='drop')  22.6 us
    all_to_all x1, waiting for transfers between devices, on_device(): lax.all_to_all(summed, 'node', split_axis=0, concat_axis=1, tiled=True)  7.33 us
    all_to_all x1, starting transfers between devices, on_device(): lax.all_to_all(loss_factors, 'node', split_axis=1, concat_axis=0, tiled=T...  7.28 us
    dot_general x1, matrix products, update(): jnp.einsum('rni,rkij->nrkj', weight_part, tiles, preferred_element_type=j...  6.55 us
    dot_general x1, matrix products, update(): jnp.einsum('nrkj,rkij->rni', picked, tiles, preferred_element_type=jnp.fl...  5.19 us
    all_to_all x1, starting transfers between devices, on_device(): lax.all_to_all(summed, 'node', split_axis=0, concat_axis=1, tiled=True)  3.63 us
  transfers between devices with their start and end apart: 3, of which 2 were waited for; matrix products, arithmetic and copies ran while one was open for 6% of the time, Pallas kernels for 0%

commit v1 on v0

v1 whole, which is shorter than its diff:
```python
import functools

import jax
import jax.numpy as jnp
from jax import lax
from jax.experimental import pallas as pl
from jax.experimental.pallas import tpu as pltpu
from jax.sharding import PartitionSpec as P


def adjoint_kernel(
    peers, epochs, group, own_ref, target_ref, occupied_ref, *refs
):
    emit_refs = refs[:peers]
    loss_refs = refs[peers : 2 * peers]
    tile_ref = refs[2 * peers]
    out_refs = refs[2 * peers + 1 : 3 * peers + 1]
    emission, collected = refs[3 * peers + 1 :]
    row, rows = pl.program_id(0), pl.num_programs(0)
    blocks_all = emission.shape[0] - 1
    side = emission.shape[2]
    slots = tile_ref.shape[1]

    @pl.when(row == 0)
    def _():
        @pl.loop(0, blocks_all // 4)
        def _(quad):
            start = pl.multiple_of(quad * 4 * epochs, 4 * epochs)
            parts = [ref[pl.ds(start, 4 * epochs), :].astype(jnp.float32) for ref in emit_refs]
            for c in range(4):
                emission[quad * 4 + c] = jnp.concatenate(
                    [part[c * epochs : (c + 1) * epochs] for part in parts], 0
                ).astype(jnp.bfloat16)

        emission[blocks_all] = jnp.zeros(emission.shape[1:], jnp.bfloat16)
        collected[...] = jnp.zeros_like(collected)

    occupied = occupied_ref[row]
    columns = [jnp.where(k < occupied, target_ref[row, k], blocks_all) for k in range(slots)]
    flux = jnp.zeros(emission.shape[1:], jnp.float32)
    for first in range(0, slots, group):
        span = range(first, first + group)
        picked = jnp.concatenate([emission[columns[k]] for k in span], 1)
        tiles = jnp.concatenate([tile_ref[0, k] for k in span], 1)
        flux += lax.dot_general(
            picked, tiles, (((1,), (1,)), ((), ())), preferred_element_type=jnp.float32
        )
    own = own_ref[0] + row
    loss = jnp.concatenate([ref[row] for ref in loss_refs], 0)
    weight = loss * (flux - emission[own].astype(jnp.float32))
    weight_b = weight.astype(jnp.bfloat16)
    collected[own] -= weight
    for first in range(0, slots, group):
        tiles = jnp.concatenate([tile_ref[0, k] for k in range(first, first + group)], 1)
        terms = jnp.dot(weight_b, tiles, preferred_element_type=jnp.float32)
        for k in range(group):
            collected[columns[first + k]] += terms[:, k * side : (k + 1) * side]

    @pl.when(row == rows - 1)
    def _():
        @pl.loop(0, blocks_all // 4)
        def _(quad):
            start = pl.multiple_of(quad * 4 * epochs, 4 * epochs)
            parts = [collected[quad * 4 + c] for c in range(4)]
            for p, ref in enumerate(out_refs):
                ref[pl.ds(start, 4 * epochs), :] = jnp.concatenate(
                    [part[p * epochs : (p + 1) * epochs] for part in parts], 0
                ).astype(jnp.bfloat16)


def adjoint_terms(own_start, targets, occupied, emit_pieces, loss_pieces, tiles):
    peers = len(emit_pieces)
    rows, slots, side = tiles.shape[:3]
    piece_rows = emit_pieces[0].shape[0]
    epochs = loss_pieces[0].shape[1]
    blocks_all = piece_rows // epochs
    samples = peers * epochs
    resident = pl.BlockSpec(memory_space=pltpu.VMEM)
    need = (
        (blocks_all + 1) * samples * side * 6
        + 2 * peers * piece_rows * side * 2
        + 4 * slots * side * side
        + peers * rows * 8 * side * 4
    )
    return pl.pallas_call(
        functools.partial(adjoint_kernel, peers, epochs, min(8, slots)),
        grid_spec=pltpu.PrefetchScalarGridSpec(
            num_scalar_prefetch=3,
            grid=(rows,),
            in_specs=[resident] * (2 * peers)
            + [pl.BlockSpec((1, slots, side, side), lambda r, *_: (r, 0, 0, 0))],
            out_specs=[resident] * peers,
            scratch_shapes=[
                pltpu.VMEM((blocks_all + 1, samples, side), jnp.bfloat16),
                pltpu.VMEM((blocks_all + 1, samples, side), jnp.float32),
            ],
        ),
        out_shape=[jax.ShapeDtypeStruct((piece_rows, side), jnp.bfloat16)] * peers,
        compiler_params=pltpu.CompilerParams(vmem_limit_bytes=need + (6 << 20)),
        cost_estimate=pl.CostEstimate(
            flops=4 * rows * slots * side * side * samples,
            bytes_accessed=rows * slots * side * side * 2,
            transcendentals=0,
        ),
    )(own_start, targets, occupied, *emit_pieces, *loss_pieces, tiles)


def on_device(
    nodes,
    scaled_kelvin,
    surface_emittance,
    loss_factors,
    gebhart_tiles,
    tile_target_index,
    tile_slots_occupied,
):
    rows, side = gebhart_tiles.shape[0], gebhart_tiles.shape[2]
    epochs, surfaces = scaled_kelvin.shape
    blocks_all = surfaces // side
    me = lax.axis_index("node")

    def send(value, step):
        return lax.ppermute(value, "node", [(i, i ^ step) for i in range(nodes)])

    def by_block(value):
        return value.reshape(-1, blocks_all, side).transpose(1, 0, 2)

    kelvin = by_block(scaled_kelvin)
    emittance = surface_emittance.reshape(blocks_all, 1, side)
    emission = (emittance * kelvin**4).astype(jnp.bfloat16).reshape(blocks_all * epochs, side)
    loss = by_block(loss_factors).reshape(nodes, rows, epochs, side)
    loss = lax.all_to_all(loss, "node", split_axis=0, concat_axis=0, tiled=True)
    loss_pieces = [lax.dynamic_index_in_dim(loss, me ^ p, 0, False) for p in range(nodes)]

    far = range(nodes - 2, 0, -2)
    emit = {0: emission}
    for p in far:
        emit[p] = send(emission, p)
    emit[1] = send(emission, 1)
    for p in far:
        emit[p ^ 1] = send(emit[p], 1)

    terms = adjoint_terms(
        (me * rows).astype(jnp.int32)[None],
        tile_target_index,
        tile_slots_occupied,
        [emit[p] for p in range(nodes)],
        loss_pieces,
        gebhart_tiles,
    )

    arrived = {p: send(terms[p ^ 1], 1) for p in [*far, 0]}
    paired = {p: terms[p].astype(jnp.float32) + arrived[p].astype(jnp.float32) for p in [*far, 0]}
    total = paired[0]
    for p in far:
        total += send(paired[p].astype(jnp.bfloat16), p).astype(jnp.float32)
    adjoint = total.reshape(blocks_all, epochs, side)
    result = 4.0 * emittance * kelvin**3 * adjoint
    return result.transpose(1, 0, 2).reshape(epochs, surfaces)


def solution(mesh):
    nodes = mesh.shape["node"]
    assert nodes & (nodes - 1) == 0
    placed = (
        P(("grp", "node", "tm"), None),
        P("grp"),
        P(("grp", "node", "tm"), None),
        P(("grp", "node"), None, None, None),
        P(("grp", "node"), None),
        P(("grp", "node")),
    )
    return jax.shard_map(
        functools.partial(on_device, nodes),
        mesh=mesh,
        in_specs=placed,
        out_specs=P(("grp", "node", "tm"), None),
        check_vma=False,
    )
```

time: 170 us -> 51.9 us (0.31)
  waiting for transfers between devices: 70.7 us -> 9.32 us
  blocking collectives: 31.9 us -> 0 us
  other arithmetic: 26.8 us -> 1.76 us
  starting transfers between devices: 10.9 us -> 25.5 us
  between operations: 13.5 us -> 0.08 us
  matrix products: 11.7 us -> 0 us
  Pallas kernels: 0 us -> 8.5 us
  local copies, waits for them, and re-layouts: 3.74 us -> 6.43 us
    reduce_scatter x1 -> x0, waiting for transfers between devices: 63.4 us -> none  [on_device(): lax.psum_scatter(collected.reshape(sample_total, surface_range).astype(jn...]
    all_gather x1 -> x0, blocking collectives: 31.9 us -> none  [on_device(): panel_rows = lax.all_gather(radiant_output, 'node', axis=0, tiled=True)]
    scatter-add x1 -> x0, other arithmetic: 22.6 us -> none  [update(): return running.at[:, targets, :].add(contrib, mode='drop')]
    ppermute x0 -> x14, starting transfers between devices: none -> 18.2 us  [send(): return lax.ppermute(value, 'node', [(i, i ^ step) for i in range(nodes)])]
    dot_general x2 -> x0, matrix products: 11.7 us -> none  [the longest x1 6.55 us: update(): jnp.einsum('rni,rkij->nrkj', weight_part, tiles, preferred_element_type=j...]
    ppermute x0 -> x14, waiting for transfers between devices: none -> 9.32 us  [send(): return lax.ppermute(value, 'node', [(i, i ^ step) for i in range(nodes)])]
    pallas_call x0 -> x1, Pallas kernels: none -> 8.5 us  [adjoint_terms(): pl.pallas_call(functools.partial(adjoint_kernel, peers, epochs, min(8, sl...]
    all_to_all x2 -> x1, waiting for transfers between devices: 7.33 us -> 0.01 us  [on_device(): loss = lax.all_to_all(loss, 'node', split_axis=0, concat_axis=0, tiled=True)]
  transfers between devices with their start and end apart: 3 -> 15, of which waited for: 2 -> 7; matrix products, arithmetic and copies ran while one was open for 6% -> 2% of each run, Pallas kernels for 0% -> 0%
where the time goes in v1:
time: 51.9 us; the launch traced here: 51.6 us
  starting transfers between devices  25.5 us (49%)
  waiting for transfers between devices  9.32 us (18%)
  Pallas kernels  8.5 us (16%)
  local copies, waits for them, and re-layouts  6.43 us (12%)
  other arithmetic  1.76 us (3%)
    ppermute x14, starting transfers between devices, send(): return lax.ppermute(value, 'node', [(i, i ^ step) for i in range(nodes)])  18.2 us
    ppermute x14, waiting for transfers between devices, send(): return lax.ppermute(value, 'node', [(i, i ^ step) for i in range(nodes)])  9.32 us
    pallas_call x1, Pallas kernels, adjoint_terms(): pl.pallas_call(functools.partial(adjoint_kernel, peers, epochs, min(8, sl...  8.5 us
    all_to_all x1, starting transfers between devices, on_device(): loss = lax.all_to_all(loss, 'node', split_axis=0, concat_axis=0, tiled=True)  7.28 us
    unnamed x11, local copies, waits for them, and re-layouts  5.68 us
  transfers between devices with their start and end apart: 15, of which 7 were waited for; matrix products, arithmetic and copies ran while one was open for 2% of the time, Pallas kernels for 0%

profile of v1, /device:TPU:0, one launch (start us, length us, event | category | flops | bytes accessed | tf_op | source)
XLA Modules:
  0.0 51.6 jit_solution(448633755354939623)
XLA Ops:
  0.0 0.9 %copy.12 = f32[1,4,64,128]{3,2,1,0:T(8,128)S(1)} copy(f32[1,4,64,128]{3,1,2,0:T(4,128)} %bitcast.46) | data formatting | bytes 262144
  1.0 0.7 %copy.8 = f32[64,4,128]{2,1,0:T(4,128)} copy(f32[64,4,128]{2,0,1:T(8,128)S(1)} %bitcast.44) | data formatting | bytes 262144 | tf_op jit(solution)/shard_map/transpose | solution.py:126
  1.7 7.3 %all-to-all-start = ((f32[8,8,4,128]{3,2,1,0:T(4,128)}), f32[8,8,4,128]{3,2,1,0:T(4,128)S(1)}, u32[]{:S(2)}, u32[]{:S(2)}) async-start(f32[8,8,4,128]{3,2,1,0:T(4,128)} %bitcast.6), calls=%async_computation | async-start | bytes 262144 | tf_op jit(solution)/shard_map/all_to_all | solution.py:132
  9.0 0.9 %fusion.4 = bf16[64,4,128]{2,1,0:T(4,128)(2,1)S(1)} fusion(f32[4,8192]{1,0:T(4,128)} %param.6, f32[64,128]{1,0:T(8,128)} %bitcast.45), kind=kLoop, calls=%fused_computation.6 | loop fusion | flops 131072 | bytes 229376 | tf_op jit(solution)/shard_map/convert_element_type | solution.py:130
  9.9 2.1 %collective-permute-start.1 = (bf16[256,128]{1,0:T(8,128)(2,1)S(1)}, bf16[256,128]{1,0:T(8,128)(2,1)S(1)}, u32[]{:S(2)}, u32[]{:S(2)}) collective-permute-start(bf16[256,128]{1,0:T(8,128)(2,1)S(1)} %bitcast.38), channel_id=1, source_target_pairs={{0,4},{2,6},{4,0},{6,2},{8,12},{10,14},{12,8},{14,10},{1,5},{3,7},... | collective-permute-start | bytes 196616 | tf_op jit(solution)/shard_map/ppermute | solution.py:123
  12.0 2.4 %collective-permute-start.3 = (bf16[256,128]{1,0:T(8,128)(2,1)S(1)}, bf16[256,128]{1,0:T(8,128)(2,1)S(1)}, u32[]{:S(2)}, u32[]{:S(2)}) collective-permute-start(bf16[256,128]{1,0:T(8,128)(2,1)S(1)} %bitcast.39), channel_id=1, source_target_pairs={{0,8},{2,10},{4,12},{6,14},{8,0},{10,2},{12,4},{14,6},{1,9},{3,11}... | collective-permute-start | bytes 196616 | tf_op jit(solution)/shard_map/ppermute | solution.py:123
  14.5 1.9 %collective-permute-start = (bf16[256,128]{1,0:T(8,128)(2,1)S(1)}, bf16[256,128]{1,0:T(8,128)(2,1)S(1)}, u32[]{:S(2)}, u32[]{:S(2)}) collective-permute-start(bf16[256,128]{1,0:T(8,128)(2,1)S(1)} %bitcast.41), channel_id=1, source_target_pairs={{0,2},{2,0},{4,6},{6,4},{8,10},{10,8},{12,14},{14,12},{1,3},{3,1},... | collective-permute-start | bytes 196616 | tf_op jit(solution)/shard_map/ppermute | solution.py:123
  16.4 0.7 %collective-permute-start.2 = (bf16[256,128]{1,0:T(8,128)(2,1)S(1)}, bf16[256,128]{1,0:T(8,128)(2,1)S(1)}, u32[]{:S(2)}, u32[]{:S(2)}) collective-permute-start(bf16[256,128]{1,0:T(8,128)(2,1)S(1)} %collective-permute-done.1.refs_2_), channel_id=1, source_target_pairs={{0,2},{2,0},{4,6},{6,4},{8,10},{10,8},{12,14},{14,12},{1,3},{3,1},... | collective-permute-start | bytes 196616 | tf_op jit(solution)/shard_map/ppermute | solution.py:123
  17.1 2.6 %collective-permute-done.3.refs_4_ = bf16[256,128]{1,0:T(8,128)(2,1)S(1)} collective-permute-done((bf16[256,128]{1,0:T(8,128)(2,1)S(1)}, bf16[256,128]{1,0:T(8,128)(2,1)S(1)}, u32[]{:S(2)}, u32[]{:S(2)}) %collective-permute-start.3) | collective-permute-done | bytes 65568 | tf_op jit(solution)/shard_map/ppermute | solution.py:123
  19.6 1.4 %collective-permute-start.4 = (bf16[256,128]{1,0:T(8,128)(2,1)S(1)}, bf16[256,128]{1,0:T(8,128)(2,1)S(1)}, u32[]{:S(2)}, u32[]{:S(2)}) collective-permute-start(bf16[256,128]{1,0:T(8,128)(2,1)S(1)} %collective-permute-done.3.refs_4_), channel_id=1, source_target_pairs={{0,2},{2,0},{4,6},{6,4},{8,10},{10,8},{12,14},{14,12},{1,3},{3,1},... | collective-permute-start | bytes 196616 | tf_op jit(solution)/shard_map/ppermute | solution.py:123
  21.0 1.0 %collective-permute-start.6 = (bf16[256,128]{1,0:T(8,128)(2,1)S(1)}, bf16[256,128]{1,0:T(8,128)(2,1)S(1)}, u32[]{:S(2)}, u32[]{:S(2)}) collective-permute-start(bf16[256,128]{1,0:T(8,128)(2,1)S(1)} %collective-permute-done.5.refs_6_), channel_id=1, source_target_pairs={{0,2},{2,0},{4,6},{6,4},{8,10},{10,8},{12,14},{14,12},{1,3},{3,1},... | collective-permute-start | bytes 196616 | tf_op jit(solution)/shard_map/ppermute | solution.py:123
  22.1 1.9 %collective-permute-done.4.refs_5_ = bf16[256,128]{1,0:T(8,128)(2,1)S(1)} collective-permute-done((bf16[256,128]{1,0:T(8,128)(2,1)S(1)}, bf16[256,128]{1,0:T(8,128)(2,1)S(1)}, u32[]{:S(2)}, u32[]{:S(2)}) %collective-permute-start.4) | collective-permute-done | bytes 65568 | tf_op jit(solution)/shard_map/ppermute | solution.py:123
  23.9 1.4 %collective-permute-done.6.refs_7_ = bf16[256,128]{1,0:T(8,128)(2,1)S(1)} collective-permute-done((bf16[256,128]{1,0:T(8,128)(2,1)S(1)}, bf16[256,128]{1,0:T(8,128)(2,1)S(1)}, u32[]{:S(2)}, u32[]{:S(2)}) %collective-permute-start.6) | collective-permute-done | bytes 65568 | tf_op jit(solution)/shard_map/ppermute | solution.py:123
  25.3 3.4 %copy-done = bf16[8,32,128,128]{3,2,1,0:T(8,128)(2,1)S(1)} copy-done((bf16[8,32,128,128]{3,2,1,0:T(8,128)(2,1)S(1)}, bf16[8,32,128,128]{3,2,1,0:T(8,128)(2,1)}, u32[]{:S(2)}) %copy-start) | copy-done | bytes 8388632
  30.0 8.5 %shard_map.64 = (bf16[256,128]{1,0:T(8,128)(2,1)S(1)}, bf16[256,128]{1,0:T(8,128)(2,1)S(1)}, bf16[256,128]{1,0:T(8,128)(2,1)S(1)}, bf16[256,128]{1,0:T(8,128)(2,...) custom-call(s32[1]{0:T(128)} %bitcast.3.own_ref, ...), custom_call_target="tpu_custom_call" | custom-call | flops 536870912 | bytes 8388608 | tf_op jit(solution)/shard_map/pallas_call | solution.py:85
  38.5 1.0 %collective-permute-start.8 = (bf16[256,128]{1,0:T(8,128)(2,1)S(1)}, bf16[256,128]{1,0:T(8,128)(2,1)S(1)}, u32[]{:S(2)}, u32[]{:S(2)}) collective-permute-start(bf16[256,128]{1,0:T(8,128)(2,1)S(1)} %get-tuple-element.16), channel_id=1, source_target_pairs={{0,2},{2,0},{4,6},{6,4},{8,10},{10,8},{12,14},{14,12},{1,3},{3,1},... | collective-permute-start | bytes 196616 | tf_op jit(solution)/shard_map/ppermute | solution.py:123
  39.5 1.1 %collective-permute-start.10 = (bf16[256,128]{1,0:T(8,128)(2,1)S(1)}, bf16[256,128]{1,0:T(8,128)(2,1)S(1)}, u32[]{:S(2)}, u32[]{:S(2)}) collective-permute-start(bf16[256,128]{1,0:T(8,128)(2,1)S(1)} %get-tuple-element.18), channel_id=1, source_target_pairs={{0,2},{2,0},{4,6},{6,4},{8,10},{10,8},{12,14},{14,12},{1,3},{3,1},... | collective-permute-start | bytes 196616 | tf_op jit(solution)/shard_map/ppermute | solution.py:123
  40.6 1.0 %collective-permute-start.12 = (bf16[256,128]{1,0:T(8,128)(2,1)S(1)}, bf16[256,128]{1,0:T(8,128)(2,1)S(1)}, u32[]{:S(2)}, u32[]{:S(2)}) collective-permute-start(bf16[256,128]{1,0:T(8,128)(2,1)S(1)} %get-tuple-element.20), channel_id=1, source_target_pairs={{0,2},{2,0},{4,6},{6,4},{8,10},{10,8},{12,14},{14,12},{1,3},{3,1},... | collective-permute-start | bytes 196616 | tf_op jit(solution)/shard_map/ppermute | solution.py:123
  41.6 1.1 %collective-permute-start.7 = (bf16[256,128]{1,0:T(8,128)(2,1)S(1)}, bf16[256,128]{1,0:T(8,128)(2,1)S(1)}, u32[]{:S(2)}, u32[]{:S(2)}) collective-permute-start(bf16[256,128]{1,0:T(8,128)(2,1)S(1)} %get-tuple-element.14), channel_id=1, source_target_pairs={{0,2},{2,0},{4,6},{6,4},{8,10},{10,8},{12,14},{14,12},{1,3},{3,1},... | collective-permute-start | bytes 196616 | tf_op jit(solution)/shard_map/ppermute | solution.py:123
  42.9 2.3 %collective-permute-start.9 = (bf16[256,128]{1,0:T(8,128)(2,1)S(1)}, bf16[256,128]{1,0:T(8,128)(2,1)S(1)}, u32[]{:S(2)}, u32[]{:S(2)}) collective-permute-start(bf16[256,128]{1,0:T(8,128)(2,1)S(1)} %add_convert_fusion.2), channel_id=1, source_target_pairs={{0,12},{2,14},{4,8},{6,10},{8,4},{10,6},{12,0},{14,2},{1,13},{3,15... | collective-permute-start | bytes 196616 | tf_op jit(solution)/shard_map/ppermute | solution.py:123
  45.8 1.7 %collective-permute-start.13 = (bf16[256,128]{1,0:T(8,128)(2,1)S(1)}, bf16[256,128]{1,0:T(8,128)(2,1)S(1)}, u32[]{:S(2)}, u32[]{:S(2)}) collective-permute-start(bf16[256,128]{1,0:T(8,128)(2,1)S(1)} %add_convert_fusion), channel_id=1, source_target_pairs={{0,4},{2,6},{4,0},{6,2},{8,12},{10,14},{12,8},{14,10},{1,5},{3,7},... | collective-permute-start | bytes 196616 | tf_op jit(solution)/shard_map/ppermute | solution.py:123
  47.5 1.5 %collective-permute-done.9 = bf16[256,128]{1,0:T(8,128)(2,1)S(1)} collective-permute-done((bf16[256,128]{1,0:T(8,128)(2,1)S(1)}, bf16[256,128]{1,0:T(8,128)(2,1)S(1)}, u32[]{:S(2)}, u32[]{:S(2)}) %collective-permute-start.9) | collective-permute-done | bytes 65568 | tf_op jit(solution)/shard_map/ppermute | solution.py:123
  49.0 1.5 %collective-permute-done.11 = bf16[256,128]{1,0:T(8,128)(2,1)S(1)} collective-permute-done((bf16[256,128]{1,0:T(8,128)(2,1)S(1)}, bf16[256,128]{1,0:T(8,128)(2,1)S(1)}, u32[]{:S(2)}, u32[]{:S(2)}) %collective-permute-start.11) | collective-permute-done | bytes 65568 | tf_op jit(solution)/shard_map/ppermute | solution.py:123
  50.9 0.7 %fusion.2 = f32[4,8192]{1,0:T(4,128)} fusion(f32[64,4,128]{2,1,0:T(4,128)S(1)} %bitcast.43, f32[4,8192]{1,0:T(4,128)S(1)} %copy-done.3, f32[64,128]{1,0:T(8,128)S(1)} %broadcast_multiply_fusion), kind=kLoop, calls=%fused_computation.4 | loop fusion | flops 131072 | bytes 425984 | tf_op jit(solution)/shard_map/reshape | solution.py:159
  (27 shorter events, 2.7 us)
Async XLA Ops:
  0.0 47.5 %copy-start.4 = (f32[8192]{0:T(1024)S(1)}, f32[8192]{0:T(1024)}, u32[]{:S(2)}) copy-start(f32[8192]{0:T(1024)} %param.7) | copy-start | bytes 98308
  0.0 50.9 %copy-start.3 = (f32[4,8192]{1,0:T(4,128)S(1)}, f32[4,8192]{1,0:T(4,128)}, u32[]{:S(2)}) copy-start(f32[4,8192]{1,0:T(4,128)} %param.6) | copy-start | bytes 393220
  1.7 20.3 %all-to-all-start = ((f32[8,8,4,128]{3,2,1,0:T(4,128)}), f32[8,8,4,128]{3,2,1,0:T(4,128)S(1)}, u32[]{:S(2)}, u32[]{:S(2)}) async-start(f32[8,8,4,128]{3,2,1,0:T(4,128)} %bitcast.6), calls=%async_computation | async-start | bytes 262144 | tf_op jit(solution)/shard_map/all_to_all | solution.py:132
  9.9 6.5 %collective-permute-start.1 = (bf16[256,128]{1,0:T(8,128)(2,1)S(1)}, bf16[256,128]{1,0:T(8,128)(2,1)S(1)}, u32[]{:S(2)}, u32[]{:S(2)}) collective-permute-start(bf16[256,128]{1,0:T(8,128)(2,1)S(1)} %bitcast.38), channel_id=1, source_target_pairs={{0,4},{2,6},{4,0},{6,2},{8,12},{10,14},{12,8},{14,10},{1,5},{3,7},... | collective-permute-start | bytes 196616 | tf_op jit(solution)/shard_map/ppermute | solution.py:123
  12.0 7.6 %collective-permute-start.3 = (bf16[256,128]{1,0:T(8,128)(2,1)S(1)}, bf16[256,128]{1,0:T(8,128)(2,1)S(1)}, u32[]{:S(2)}, u32[]{:S(2)}) collective-permute-start(bf16[256,128]{1,0:T(8,128)(2,1)S(1)} %bitcast.39), channel_id=1, source_target_pairs={{0,8},{2,10},{4,12},{6,14},{8,0},{10,2},{12,4},{14,6},{1,9},{3,11}... | collective-permute-start | bytes 196616 | tf_op jit(solution)/shard_map/ppermute | solution.py:123
  14.4 6.6 %collective-permute-start.5 = (bf16[256,128]{1,0:T(8,128)(2,1)S(1)}, bf16[256,128]{1,0:T(8,128)(2,1)S(1)}, u32[]{:S(2)}, u32[]{:S(2)}) collective-permute-start(bf16[256,128]{1,0:T(8,128)(2,1)S(1)} %bitcast.40), channel_id=1, source_target_pairs={{0,12},{2,14},{4,8},{6,10},{8,4},{10,6},{12,0},{14,2},{1,13},{3,15... | collective-permute-start | bytes 196616 | tf_op jit(solution)/shard_map/ppermute | solution.py:123
  14.5 7.6 %collective-permute-start = (bf16[256,128]{1,0:T(8,128)(2,1)S(1)}, bf16[256,128]{1,0:T(8,128)(2,1)S(1)}, u32[]{:S(2)}, u32[]{:S(2)}) collective-permute-start(bf16[256,128]{1,0:T(8,128)(2,1)S(1)} %bitcast.41), channel_id=1, source_target_pairs={{0,2},{2,0},{4,6},{6,4},{8,10},{10,8},{12,14},{14,12},{1,3},{3,1},... | collective-permute-start | bytes 196616 | tf_op jit(solution)/shard_map/ppermute | solution.py:123
  16.4 5.6 %collective-permute-start.2 = (bf16[256,128]{1,0:T(8,128)(2,1)S(1)}, bf16[256,128]{1,0:T(8,128)(2,1)S(1)}, u32[]{:S(2)}, u32[]{:S(2)}) collective-permute-start(bf16[256,128]{1,0:T(8,128)(2,1)S(1)} %collective-permute-done.1.refs_2_), channel_id=1, source_target_pairs={{0,2},{2,0},{4,6},{6,4},{8,10},{10,8},{12,14},{14,12},{1,3},{3,1},... | collective-permute-start | bytes 196616 | tf_op jit(solution)/shard_map/ppermute | solution.py:123
  19.6 4.3 %collective-permute-start.4 = (bf16[256,128]{1,0:T(8,128)(2,1)S(1)}, bf16[256,128]{1,0:T(8,128)(2,1)S(1)}, u32[]{:S(2)}, u32[]{:S(2)}) collective-permute-start(bf16[256,128]{1,0:T(8,128)(2,1)S(1)} %collective-permute-done.3.refs_4_), channel_id=1, source_target_pairs={{0,2},{2,0},{4,6},{6,4},{8,10},{10,8},{12,14},{14,12},{1,3},{3,1},... | collective-permute-start | bytes 196616 | tf_op jit(solution)/shard_map/ppermute | solution.py:123
  21.0 4.3 %collective-permute-start.6 = (bf16[256,128]{1,0:T(8,128)(2,1)S(1)}, bf16[256,128]{1,0:T(8,128)(2,1)S(1)}, u32[]{:S(2)}, u32[]{:S(2)}) collective-permute-start(bf16[256,128]{1,0:T(8,128)(2,1)S(1)} %collective-permute-done.5.refs_6_), channel_id=1, source_target_pairs={{0,2},{2,0},{4,6},{6,4},{8,10},{10,8},{12,14},{14,12},{1,3},{3,1},... | collective-permute-start | bytes 196616 | tf_op jit(solution)/shard_map/ppermute | solution.py:123
  25.3 3.4 %copy-start = (bf16[8,32,128,128]{3,2,1,0:T(8,128)(2,1)S(1)}, bf16[8,32,128,128]{3,2,1,0:T(8,128)(2,1)}, u32[]{:S(2)}) copy-start(bf16[8,32,128,128]{3,2,1,0:T(8,128)(2,1)} %refs_16_.1) | copy-start | bytes 25165828
  28.7 0.7 %copy-start.1 = (s32[8,32]{1,0:T(8,128)S(1)}, s32[8,32]{1,0:T(8,128)}, u32[]{:S(2)}) copy-start(s32[8,32]{1,0:T(8,128)} %target_ref.1) | copy-start | bytes 3076
  29.4 0.7 %copy-start.2 = (s32[8]{0:T(128)S(1)}, s32[8]{0:T(128)}, u32[]{:S(2)}) copy-start(s32[8]{0:T(128)} %occupied_ref.1) | copy-start | bytes 100
  38.5 4.3 %collective-permute-start.8 = (bf16[256,128]{1,0:T(8,128)(2,1)S(1)}, bf16[256,128]{1,0:T(8,128)(2,1)S(1)}, u32[]{:S(2)}, u32[]{:S(2)}) collective-permute-start(bf16[256,128]{1,0:T(8,128)(2,1)S(1)} %get-tuple-element.16), channel_id=1, source_target_pairs={{0,2},{2,0},{4,6},{6,4},{8,10},{10,8},{12,14},{14,12},{1,3},{3,1},... | collective-permute-start | bytes 196616 | tf_op jit(solution)/shard_map/ppermute | solution.py:123
  39.5 5.6 %collective-permute-start.10 = (bf16[256,128]{1,0:T(8,128)(2,1)S(1)}, bf16[256,128]{1,0:T(8,128)(2,1)S(1)}, u32[]{:S(2)}, u32[]{:S(2)}) collective-permute-start(bf16[256,128]{1,0:T(8,128)(2,1)S(1)} %get-tuple-element.18), channel_id=1, source_target_pairs={{0,2},{2,0},{4,6},{6,4},{8,10},{10,8},{12,14},{14,12},{1,3},{3,1},... | collective-permute-start | bytes 196616 | tf_op jit(solution)/shard_map/ppermute | solution.py:123
  40.6 5.2 %collective-permute-start.12 = (bf16[256,128]{1,0:T(8,128)(2,1)S(1)}, bf16[256,128]{1,0:T(8,128)(2,1)S(1)}, u32[]{:S(2)}, u32[]{:S(2)}) collective-permute-start(bf16[256,128]{1,0:T(8,128)(2,1)S(1)} %get-tuple-element.20), channel_id=1, source_target_pairs={{0,2},{2,0},{4,6},{6,4},{8,10},{10,8},{12,14},{14,12},{1,3},{3,1},... | collective-permute-start | bytes 196616 | tf_op jit(solution)/shard_map/ppermute | solution.py:123
  41.6 6.0 %collective-permute-start.7 = (bf16[256,128]{1,0:T(8,128)(2,1)S(1)}, bf16[256,128]{1,0:T(8,128)(2,1)S(1)}, u32[]{:S(2)}, u32[]{:S(2)}) collective-permute-start(bf16[256,128]{1,0:T(8,128)(2,1)S(1)} %get-tuple-element.14), channel_id=1, source_target_pairs={{0,2},{2,0},{4,6},{6,4},{8,10},{10,8},{12,14},{14,12},{1,3},{3,1},... | collective-permute-start | bytes 196616 | tf_op jit(solution)/shard_map/ppermute | solution.py:123
  42.9 6.1 %collective-permute-start.9 = (bf16[256,128]{1,0:T(8,128)(2,1)S(1)}, bf16[256,128]{1,0:T(8,128)(2,1)S(1)}, u32[]{:S(2)}, u32[]{:S(2)}) collective-permute-start(bf16[256,128]{1,0:T(8,128)(2,1)S(1)} %add_convert_fusion.2), channel_id=1, source_target_pairs={{0,12},{2,14},{4,8},{6,10},{8,4},{10,6},{12,0},{14,2},{1,13},{3,15... | collective-permute-start | bytes 196616 | tf_op jit(solution)/shard_map/ppermute | solution.py:123
  45.2 5.3 %collective-permute-start.11 = (bf16[256,128]{1,0:T(8,128)(2,1)S(1)}, bf16[256,128]{1,0:T(8,128)(2,1)S(1)}, u32[]{:S(2)}, u32[]{:S(2)}) collective-permute-start(bf16[256,128]{1,0:T(8,128)(2,1)S(1)} %add_convert_fusion.1), channel_id=1, source_target_pairs={{0,8},{2,10},{4,12},{6,14},{8,0},{10,2},{12,4},{14,6},{1,9},{3,11}... | collective-permute-start | bytes 196616 | tf_op jit(solution)/shard_map/ppermute | solution.py:123
  45.8 5.0 %collective-permute-start.13 = (bf16[256,128]{1,0:T(8,128)(2,1)S(1)}, bf16[256,128]{1,0:T(8,128)(2,1)S(1)}, u32[]{:S(2)}, u32[]{:S(2)}) collective-permute-start(bf16[256,128]{1,0:T(8,128)(2,1)S(1)} %add_convert_fusion), channel_id=1, source_target_pairs={{0,4},{2,6},{4,0},{6,2},{8,12},{10,14},{12,8},{14,10},{1,5},{3,7},... | collective-permute-start | bytes 196616 | tf_op jit(solution)/shard_map/ppermute | solution.py:123

commit v2 on v0

v2 whole, which is shorter than its diff:
```python
import functools

import jax
import jax.numpy as jnp
from jax import lax
from jax.experimental import pallas as pl
from jax.experimental.pallas import tpu as pltpu
from jax.sharding import PartitionSpec as P

RESIDENT = pl.BlockSpec(memory_space=pltpu.VMEM)
F32, BF16 = jnp.float32, jnp.bfloat16


def halves(value):
    high = value.astype(BF16)
    return high, (value - high.astype(F32)).astype(BF16)


def prepare_kernel(
    far, rows, kelvin_ref, emittance_ref, loss_ref, target_ref, occupied_ref, *out_refs
):
    z_refs = out_refs[: len(far)]
    own_ref, pair_ref, scale_ref, table_ref = out_refs[len(far) :]
    epochs = kelvin_ref.shape[0]
    blocks_all, side = emittance_ref.shape
    me = lax.axis_index("node")
    part = rows * epochs
    wide = blocks_all * epochs

    for first in range(0, blocks_all, 4):
        emissions, scales = [], []
        for c in range(first, first + 4):
            kelvin = kelvin_ref[:, c * side : (c + 1) * side]
            emittance = emittance_ref[c : c + 1, :]
            square = kelvin * kelvin
            emissions.append(emittance * (square * square))
            scales.append(4.0 * emittance * (square * kelvin))
        emission = jnp.concatenate(emissions, 0).astype(BF16)
        span = slice(first * epochs, (first + 4) * epochs)
        scale_ref[span, :] = jnp.concatenate(scales, 0)
        own_ref[span, :] = emission
        pair_ref[span, :] = emission
        for ref in z_refs:
            ref[2 * part + first * epochs : 2 * part + (first + 4) * epochs, :] = emission

    def put_loss(ref, start, peer):
        width = rows * side
        loss = loss_ref[:, pl.ds(pl.multiple_of(peer * width, width), width)]
        loss = jnp.concatenate([loss[:, r * side : (r + 1) * side] for r in range(rows)], 0)
        high, low = halves(loss)
        ref[start : start + part, :] = high
        ref[start + part : start + 2 * part, :] = low

    put_loss(own_ref, wide, me)
    put_loss(pair_ref, wide, me ^ 1)
    for p, ref in zip(far, z_refs):
        put_loss(ref, 0, me ^ p)
        put_loss(ref, 2 * part + wide, me ^ p ^ 1)

    slots = target_ref.shape[1]
    slot = lax.broadcasted_iota(jnp.int32, (1, slots), 1)
    for r in range(rows):
        table_ref[r : r + 1, :] = jnp.where(
            slot < occupied_ref[r], target_ref[r : r + 1, :], blocks_all
        )


def prepare(far, scaled_kelvin, surface_emittance, loss_factors, targets, occupied, side):
    epochs, surfaces = scaled_kelvin.shape
    rows = targets.shape[0]
    blocks_all = surfaces // side
    part, wide = 2 * rows * epochs, blocks_all * epochs
    held = [
        pltpu.with_memory_space_constraint(value, pltpu.HBM)
        for value in (
            scaled_kelvin,
            surface_emittance.reshape(blocks_all, side),
            loss_factors,
            targets,
            occupied,
        )
    ]
    whole = lambda value: pl.BlockSpec(value.shape, lambda i: (0,) * value.ndim)
    return pl.pallas_call(
        functools.partial(prepare_kernel, far, rows),
        grid=(1,),
        in_specs=[whole(value) for value in held[:4]] + [pl.BlockSpec(memory_space=pltpu.SMEM)],
        out_specs=[RESIDENT] * (len(far) + 4),
        out_shape=[jax.ShapeDtypeStruct((wide + 2 * part, side), BF16)] * len(far)
        + [jax.ShapeDtypeStruct((wide + part, side), BF16)] * 2
        + [jax.ShapeDtypeStruct((wide, side), F32), jax.ShapeDtypeStruct(targets.shape, jnp.int32)],
        compiler_params=pltpu.CompilerParams(vmem_limit_bytes=24 << 20),
    )(*held)


def adjoint_kernel(peers, rows, epochs, group, table_ref, *refs):
    piece_refs, tiles_ref = refs[:peers], refs[peers]
    out_refs = refs[peers + 1 : 2 * peers + 1]
    tiles, emission, loss, collected, sems = refs[2 * peers + 1 :]
    blocks_all, samples, side = emission.shape[0] - 1, emission.shape[1], emission.shape[2]
    slots = tiles.shape[1]
    part, wide = rows * epochs, blocks_all * epochs
    me = lax.axis_index("node")

    loads = [pltpu.make_async_copy(tiles_ref.at[r], tiles.at[r], sems.at[r]) for r in range(rows)]
    for load in loads:
        load.start()

    emit_at = [2 * part if p and not p & 1 else 0 for p in range(peers)]
    loss_at = [0 if p and not p & 1 else wide for p in range(peers)]

    @pl.loop(0, blocks_all // 4)
    def _(quad):
        step = pl.multiple_of(quad * 4 * epochs, 4 * epochs)
        parts = [
            ref[pl.ds(start + step, 4 * epochs), :].astype(F32)
            for ref, start in zip(piece_refs, emit_at)
        ]
        for c in range(4):
            emission[quad * 4 + c] = jnp.concatenate(
                [part[c * epochs : (c + 1) * epochs] for part in parts], 0
            ).astype(BF16)

    for first in range(0, rows, 4):
        parts = []
        for ref, start in zip(piece_refs, loss_at):
            span = slice(start + first * epochs, start + (first + 4) * epochs)
            rest = slice(span.start + part, span.stop + part)
            parts.append(ref[span, :].astype(F32) + ref[rest, :].astype(F32))
        for c in range(4):
            loss[first + c] = jnp.concatenate(
                [value[c * epochs : (c + 1) * epochs] for value in parts], 0
            )

    emission[blocks_all] = jnp.zeros(emission.shape[1:], BF16)
    collected[...] = jnp.zeros_like(collected)

    for block_rows in [range(first, first + 4) for first in range(0, rows, 4)]:
        for r in block_rows:
            loads[r].wait()
        weights = {}
        for r in block_rows:
            flux = jnp.zeros((samples, side), F32)
            for first in range(0, slots, group):
                span = range(first, first + group)
                picked = jnp.concatenate([emission[table_ref[r, k]] for k in span], 1)
                stored = jnp.concatenate([tiles[r, k] for k in span], 1)
                flux += lax.dot_general(
                    picked, stored, (((1,), (1,)), ((), ())), preferred_element_type=F32
                )
            own = me * rows + r
            weight = loss[r] * (flux - emission[own].astype(F32))
            weights[r] = weight.astype(BF16)
            collected[own] -= weight
        for r in block_rows:
            for first in range(0, slots, group):
                stored = jnp.concatenate([tiles[r, k] for k in range(first, first + group)], 1)
                terms = jnp.dot(weights[r], stored, preferred_element_type=F32)
                for k in range(group):
                    collected[table_ref[r, first + k]] += terms[:, k * side : (k + 1) * side]

    @pl.loop(0, blocks_all // 4)
    def _(quad):
        step = pl.multiple_of(quad * 4 * epochs, 4 * epochs)
        parts = [collected[quad * 4 + c] for c in range(4)]
        for p, ref in enumerate(out_refs):
            ref[pl.ds(step, 4 * epochs), :] = jnp.concatenate(
                [part[p * epochs : (p + 1) * epochs] for part in parts], 0
            ).astype(BF16)

    for first in range(0, rows, 4):
        parts = [collected[me * rows + first + c] for c in range(4)]
        for p, ref in enumerate(out_refs):
            full = jnp.concatenate([part[p * epochs : (p + 1) * epochs] for part in parts], 0)
            ref[wide + first * epochs : wide + (first + 4) * epochs, :] = halves(full)[1]


def adjoint_terms(table, pieces, tiles, epochs, blocks_all):
    peers = len(pieces)
    rows, slots, side = tiles.shape[:3]
    samples = peers * epochs
    out_rows = (blocks_all + rows) * epochs
    need = (
        (blocks_all + 1) * samples * side * 6
        + 2 * peers * out_rows * side * 2
        + rows * slots * side * side * 2
        + rows * samples * side * 4
    )
    return pl.pallas_call(
        functools.partial(adjoint_kernel, peers, rows, epochs, min(8, slots)),
        in_specs=[pl.BlockSpec(memory_space=pltpu.SMEM)]
        + [RESIDENT] * peers
        + [pl.BlockSpec(memory_space=pl.ANY)],
        out_specs=[RESIDENT] * peers,
        scratch_shapes=[
            pltpu.VMEM(tiles.shape, BF16),
            pltpu.VMEM((blocks_all + 1, samples, side), BF16),
            pltpu.VMEM((rows, samples, side), F32),
            pltpu.VMEM((blocks_all + 1, samples, side), F32),
            pltpu.SemaphoreType.DMA((rows,)),
        ],
        out_shape=[jax.ShapeDtypeStruct((out_rows, side), BF16)] * peers,
        compiler_params=pltpu.CompilerParams(vmem_limit_bytes=need + (6 << 20)),
        cost_estimate=pl.CostEstimate(
            flops=4 * rows * slots * side * side * samples,
            bytes_accessed=rows * slots * side * side * 2,
            transcendentals=0,
        ),
    )(table, *pieces, pltpu.with_memory_space_constraint(tiles, pltpu.HBM))


def finish_kernel(steps, rows, epochs, scale_ref, *refs):
    sum_refs, out_ref, total = refs[: len(steps)], refs[-2], refs[-1]
    wide, side = total.shape
    part = 2 * rows * epochs
    pair = lax.axis_index("node") // 2
    total[...] = sum(ref[:wide, :].astype(F32) for ref in sum_refs)
    for p, ref in zip(steps, sum_refs):
        span = pl.ds(pl.multiple_of((pair ^ (p // 2)) * part, part), part)
        total[span, :] += ref[wide:, :].astype(F32)
    for c in range(wide // epochs):
        span = slice(c * epochs, (c + 1) * epochs)
        out_ref[:, c * side : (c + 1) * side] = scale_ref[span, :] * total[span, :]


def finish(steps, rows, epochs, scale, sums):
    wide, side = scale.shape
    return pl.pallas_call(
        functools.partial(finish_kernel, steps, rows, epochs),
        in_specs=[RESIDENT] * (1 + len(sums)),
        out_specs=RESIDENT,
        scratch_shapes=[pltpu.VMEM((wide, side), F32)],
        out_shape=jax.ShapeDtypeStruct((epochs, wide // epochs * side), F32),
        compiler_params=pltpu.CompilerParams(vmem_limit_bytes=24 << 20),
    )(scale, *sums)


def add_neighbour(me, wide, mine, theirs):
    total = mine[:wide].astype(F32) + theirs[:wide].astype(F32)
    low_mine, low_theirs = mine[wide:].astype(F32), theirs[wide:].astype(F32)
    odd = me % 2 == 1
    low = jnp.concatenate(
        [jnp.where(odd, low_theirs, low_mine), jnp.where(odd, low_mine, low_theirs)], 0
    )
    start = (me // 2) * low.shape[0]
    high, low = halves(lax.dynamic_slice_in_dim(total, start, low.shape[0], 0) + low)
    total = lax.dynamic_update_slice_in_dim(total.astype(BF16), high, start, 0)
    return jnp.concatenate([total, low], 0)


def on_device(
    nodes,
    scaled_kelvin,
    surface_emittance,
    loss_factors,
    gebhart_tiles,
    tile_target_index,
    tile_slots_occupied,
):
    rows, side = gebhart_tiles.shape[0], gebhart_tiles.shape[2]
    epochs, surfaces = scaled_kelvin.shape
    blocks_all = surfaces // side
    wide = blocks_all * epochs
    me = lax.axis_index("node")

    def send(value, step):
        return lax.ppermute(value, "node", [(i, i ^ step) for i in range(nodes)])

    far = tuple(range(nodes - 2, 0, -2))
    *along_z, own, pair, scale, table = prepare(
        far,
        scaled_kelvin,
        surface_emittance,
        loss_factors,
        tile_target_index,
        tile_slots_occupied,
        side,
    )
    pieces = {0: own}
    for p, piece in zip(far, along_z):
        pieces[p] = send(piece, p)
    pieces[1] = send(pair, 1)
    for p in far:
        pieces[p ^ 1] = send(pieces[p][2 * rows * epochs :], 1)

    terms = adjoint_terms(
        table, [pieces[p] for p in range(nodes)], gebhart_tiles, epochs, blocks_all
    )

    steps = (*far, 0)
    arrived = {p: send(terms[p ^ 1], 1) for p in steps}
    paired = {p: add_neighbour(me, wide, terms[p], arrived[p]) for p in steps}
    sums = [send(paired[p], p) for p in far] + [paired[0]]
    return finish(steps, rows, epochs, scale, sums)


def solution(mesh):
    nodes = mesh.shape["node"]
    assert nodes & (nodes - 1) == 0
    placed = (
        P(("grp", "node", "tm"), None),
        P("grp"),
        P(("grp", "node", "tm"), None),
        P(("grp", "node"), None, None, None),
        P(("grp", "node"), None),
        P(("grp", "node")),
    )
    return jax.shard_map(
        functools.partial(on_device, nodes),
        mesh=mesh,
        in_specs=placed,
        out_specs=P(("grp", "node", "tm"), None),
        check_vma=False,
    )
```

time: 170 us -> 43.7 us (0.26)
  waiting for transfers between devices: 70.7 us -> 15.6 us
  blocking collectives: 31.9 us -> 0 us
  other arithmetic: 26.8 us -> 0.29 us
  between operations: 13.5 us -> 0.17 us
  matrix products: 11.7 us -> 0 us
  Pallas kernels: 0 us -> 9.44 us
  starting transfers between devices: 10.9 us -> 17.9 us
  local copies, waits for them, and re-layouts: 3.74 us -> 0.02 us
    reduce_scatter x1 -> x0, waiting for transfers between devices: 63.4 us -> none  [on_device(): lax.psum_scatter(collected.reshape(sample_total, surface_range).astype(jn...]
    all_gather x1 -> x0, blocking collectives: 31.9 us -> none  [on_device(): panel_rows = lax.all_gather(radiant_output, 'node', axis=0, tiled=True)]
    scatter-add x1 -> x0, other arithmetic: 22.6 us -> none  [update(): return running.at[:, targets, :].add(contrib, mode='drop')]
    ppermute x0 -> x14, starting transfers between devices: none -> 17.9 us  [send(): return lax.ppermute(value, 'node', [(i, i ^ step) for i in range(nodes)])]
    ppermute x0 -> x14, waiting for transfers between devices: none -> 15.6 us  [send(): return lax.ppermute(value, 'node', [(i, i ^ step) for i in range(nodes)])]
    dot_general x2 -> x0, matrix products: 11.7 us -> none  [the longest x1 6.55 us: update(): jnp.einsum('rni,rkij->nrkj', weight_part, tiles, preferred_element_type=j...]
    all_to_all x2 -> x0, starting transfers between devices: 10.9 us -> none  [the longest x1 7.28 us: on_device(): lax.all_to_all(loss_factors, 'node', split_axis=1, concat_axis=0, tiled=T...]
    pallas_call x0 -> x3, Pallas kernels: none -> 9.44 us  [the longest x1 7.6 us: adjoint_terms(): pl.pallas_call(functools.partial(adjoint_kernel, peers, rows, epochs, min...]
  transfers between devices with their start and end apart: 3 -> 14, of which waited for: 2 -> 8; matrix products, arithmetic and copies ran while one was open for 6% -> 1% of each run, Pallas kernels for 0% -> 0%
where the time goes in v2:
time: 43.7 us; the launch traced here: 43.5 us
  starting transfers between devices  17.9 us (41%)
  waiting for transfers between devices  15.6 us (36%)
  Pallas kernels  9.44 us (22%)
    ppermute x14, starting transfers between devices, send(): return lax.ppermute(value, 'node', [(i, i ^ step) for i in range(nodes)])  17.9 us
    ppermute x14, waiting for transfers between devices, send(): return lax.ppermute(value, 'node', [(i, i ^ step) for i in range(nodes)])  15.6 us
    pallas_call x1, Pallas kernels, adjoint_terms(): pl.pallas_call(functools.partial(adjoint_kernel, peers, rows, epochs, min...  7.6 us
    pallas_call x1, Pallas kernels, prepare(): pl.pallas_call(functools.partial(prepare_kernel, far, rows), grid=(1,), i...  1.09 us
  transfers between devices with their start and end apart: 14, of which 8 were waited for; matrix products, arithmetic and copies ran while one was open for 1% of the time, Pallas kernels for 0%

profile of v2, /device:TPU:0, one launch (start us, length us, event | category | flops | bytes accessed | tf_op | source)
XLA Modules:
  0.0 43.5 jit_solution(5421100789557941687)
XLA Ops:
  0.0 1.1 %shard_map.64 = (bf16[384,128]{1,0:T(8,128)(2,1)S(1)}, bf16[384,128]{1,0:T(8,128)(2,1)S(1)}, bf16[384,128]{1,0:T(8,128)(2,1)S(1)}, bf16[320,128]{1,0:T(8,128)(2,...) custom-call(f32[4,8192]{1,0:T(4,128)} %kelvin_ref.1, f32[64,128]{1,0:T(8,128)} %bitcast.1, ...), custom_call_target="tpu_custom_call" | custom-call | tf_op jit(solution)/shard_map/pallas_call | solution.py:84
  1.1 3.1 %collective-permute-start.1 = (bf16[384,128]{1,0:T(8,128)(2,1)S(1)}, bf16[384,128]{1,0:T(8,128)(2,1)S(1)}, u32[]{:S(2)}, u32[]{:S(2)}) collective-permute-start(bf16[384,128]{1,0:T(8,128)(2,1)S(1)} %get-tuple-element.24), channel_id=1, source_target_pairs={{0,4},{2,6},{4,0},{6,2},{8,12},{10,14},{12,8},{14,10},{1,5},{3,7},... | collective-permute-start | bytes 294920 | tf_op jit(solution)/shard_map/ppermute | solution.py:267
  4.2 2.6 %collective-permute-start.3 = (bf16[384,128]{1,0:T(8,128)(2,1)S(1)}, bf16[384,128]{1,0:T(8,128)(2,1)S(1)}, u32[]{:S(2)}, u32[]{:S(2)}) collective-permute-start(bf16[384,128]{1,0:T(8,128)(2,1)S(1)} %get-tuple-element.25), channel_id=1, source_target_pairs={{0,8},{2,10},{4,12},{6,14},{8,0},{10,2},{12,4},{14,6},{1,9},{3,11}... | collective-permute-start | bytes 294920 | tf_op jit(solution)/shard_map/ppermute | solution.py:267
  6.8 1.7 %collective-permute-start = (bf16[320,128]{1,0:T(8,128)(2,1)S(1)}, bf16[320,128]{1,0:T(8,128)(2,1)S(1)}, u32[]{:S(2)}, u32[]{:S(2)}) collective-permute-start(bf16[320,128]{1,0:T(8,128)(2,1)S(1)} %get-tuple-element.23), channel_id=1, source_target_pairs={{0,2},{2,0},{4,6},{6,4},{8,10},{10,8},{12,14},{14,12},{1,3},{3,1},... | collective-permute-start | bytes 245768 | tf_op jit(solution)/shard_map/ppermute | solution.py:267
  8.5 0.4 collective-permute-start.2
  8.9 5.7 %collective-permute-done.3.refs_4_ = bf16[384,128]{1,0:T(8,128)(2,1)S(1)} collective-permute-done((bf16[384,128]{1,0:T(8,128)(2,1)S(1)}, bf16[384,128]{1,0:T(8,128)(2,1)S(1)}, u32[]{:S(2)}, u32[]{:S(2)}) %collective-permute-start.3) | collective-permute-done | bytes 98336 | tf_op jit(solution)/shard_map/ppermute | solution.py:267
  14.6 1.5 %collective-permute-start.4 = (bf16[320,128]{1,0:T(8,128)(2,1)S(1)}, bf16[320,128]{1,0:T(8,128)(2,1)S(1)}, u32[]{:S(2)}, u32[]{:S(2)}) collective-permute-start(bf16[320,128]{1,0:T(8,128)(2,1)S(1)} %slice.77), channel_id=1, source_target_pairs={{0,2},{2,0},{4,6},{6,4},{8,10},{10,8},{12,14},{14,12},{1,3},{3,1},... | collective-permute-start | bytes 245768 | tf_op jit(solution)/shard_map/ppermute | solution.py:267
  16.2 0.6 %collective-permute-start.6 = (bf16[320,128]{1,0:T(8,128)(2,1)S(1)}, bf16[320,128]{1,0:T(8,128)(2,1)S(1)}, u32[]{:S(2)}, u32[]{:S(2)}) collective-permute-start(bf16[320,128]{1,0:T(8,128)(2,1)S(1)} %slice.78), channel_id=1, source_target_pairs={{0,2},{2,0},{4,6},{6,4},{8,10},{10,8},{12,14},{14,12},{1,3},{3,1},... | collective-permute-start | bytes 245768 | tf_op jit(solution)/shard_map/ppermute | solution.py:267
  16.7 2.3 %collective-permute-done.4.refs_5_ = bf16[320,128]{1,0:T(8,128)(2,1)S(1)} collective-permute-done((bf16[320,128]{1,0:T(8,128)(2,1)S(1)}, bf16[320,128]{1,0:T(8,128)(2,1)S(1)}, u32[]{:S(2)}, u32[]{:S(2)}) %collective-permute-start.4) | collective-permute-done | bytes 81952 | tf_op jit(solution)/shard_map/ppermute | solution.py:267
  19.1 1.6 %collective-permute-done.6.refs_7_ = bf16[320,128]{1,0:T(8,128)(2,1)S(1)} collective-permute-done((bf16[320,128]{1,0:T(8,128)(2,1)S(1)}, bf16[320,128]{1,0:T(8,128)(2,1)S(1)}, u32[]{:S(2)}, u32[]{:S(2)}) %collective-permute-start.6) | collective-permute-done | bytes 81952 | tf_op jit(solution)/shard_map/ppermute | solution.py:267
  20.7 7.6 %shard_map.65 = (bf16[288,128]{1,0:T(8,128)(2,1)S(1)}, bf16[288,128]{1,0:T(8,128)(2,1)S(1)}, bf16[288,128]{1,0:T(8,128)(2,1)S(1)}, bf16[288,128]{1,0:T(8,128)(2,...) custom-call(s32[8,32]{1,0:T(8,128)S(1)} %get-tuple-element.21.table_, ...), custom_call_target="tpu_custom_call" | custom-call | flops 536870912 | bytes 8388608 | tf_op jit(solution)/shard_map/pallas_call | solution.py:189
  28.3 0.8 %collective-permute-start.11 = (bf16[288,128]{1,0:T(8,128)(2,1)S(1)}, bf16[288,128]{1,0:T(8,128)(2,1)S(1)}, u32[]{:S(2)}, u32[]{:S(2)}) collective-permute-start(bf16[288,128]{1,0:T(8,128)(2,1)S(1)} %get-tuple-element.32), channel_id=1, source_target_pairs={{0,2},{2,0},{4,6},{6,4},{8,10},{10,8},{12,14},{14,12},{1,3},{3,1},... | collective-permute-start | bytes 221192 | tf_op jit(solution)/shard_map/ppermute | solution.py:267
  29.1 1.3 %collective-permute-start.13 = (bf16[288,128]{1,0:T(8,128)(2,1)S(1)}, bf16[288,128]{1,0:T(8,128)(2,1)S(1)}, u32[]{:S(2)}, u32[]{:S(2)}) collective-permute-start(bf16[288,128]{1,0:T(8,128)(2,1)S(1)} %get-tuple-element.34), channel_id=1, source_target_pairs={{0,2},{2,0},{4,6},{6,4},{8,10},{10,8},{12,14},{14,12},{1,3},{3,1},... | collective-permute-start | bytes 221192 | tf_op jit(solution)/shard_map/ppermute | solution.py:267
  30.4 0.8 %collective-permute-start.9 = (bf16[288,128]{1,0:T(8,128)(2,1)S(1)}, bf16[288,128]{1,0:T(8,128)(2,1)S(1)}, u32[]{:S(2)}, u32[]{:S(2)}) collective-permute-start(bf16[288,128]{1,0:T(8,128)(2,1)S(1)} %get-tuple-element.30), channel_id=1, source_target_pairs={{0,2},{2,0},{4,6},{6,4},{8,10},{10,8},{12,14},{14,12},{1,3},{3,1},... | collective-permute-start | bytes 221192 | tf_op jit(solution)/shard_map/ppermute | solution.py:267
  31.1 1.3 %collective-permute-start.7 = (bf16[288,128]{1,0:T(8,128)(2,1)S(1)}, bf16[288,128]{1,0:T(8,128)(2,1)S(1)}, u32[]{:S(2)}, u32[]{:S(2)}) collective-permute-start(bf16[288,128]{1,0:T(8,128)(2,1)S(1)} %get-tuple-element.28), channel_id=1, source_target_pairs={{0,2},{2,0},{4,6},{6,4},{8,10},{10,8},{12,14},{14,12},{1,3},{3,1},... | collective-permute-start | bytes 221192 | tf_op jit(solution)/shard_map/ppermute | solution.py:267
  32.4 0.3 collective-permute-done.11
  32.8 0.9 %collective-permute-start.12 = (bf16[320,128]{1,0:T(8,128)(2,1)S(1)}, bf16[320,128]{1,0:T(8,128)(2,1)S(1)}, u32[]{:S(2)}, u32[]{:S(2)}) collective-permute-start(bf16[320,128]{1,0:T(8,128)(2,1)S(1)} %pad_maximum_fusion.2), channel_id=1, source_target_pairs={{0,4},{2,6},{4,0},{6,2},{8,12},{10,14},{12,8},{14,10},{1,5},{3,7},... | collective-permute-start | bytes 245768 | tf_op jit(solution)/shard_map/ppermute | solution.py:267
  33.7 1.1 %collective-permute-done.9 = bf16[288,128]{1,0:T(8,128)(2,1)S(1)} collective-permute-done((bf16[288,128]{1,0:T(8,128)(2,1)S(1)}, bf16[288,128]{1,0:T(8,128)(2,1)S(1)}, u32[]{:S(2)}, u32[]{:S(2)}) %collective-permute-start.9) | collective-permute-done | bytes 73760 | tf_op jit(solution)/shard_map/ppermute | solution.py:267
  34.8 1.3 %collective-permute-start.10 = (bf16[320,128]{1,0:T(8,128)(2,1)S(1)}, bf16[320,128]{1,0:T(8,128)(2,1)S(1)}, u32[]{:S(2)}, u32[]{:S(2)}) collective-permute-start(bf16[320,128]{1,0:T(8,128)(2,1)S(1)} %pad_maximum_fusion.1), channel_id=1, source_target_pairs={{0,8},{2,10},{4,12},{6,14},{8,0},{10,2},{12,4},{14,6},{1,9},{3,11}... | collective-permute-start | bytes 245768 | tf_op jit(solution)/shard_map/ppermute | solution.py:267
  36.3 1.8 %collective-permute-start.8 = (bf16[320,128]{1,0:T(8,128)(2,1)S(1)}, bf16[320,128]{1,0:T(8,128)(2,1)S(1)}, u32[]{:S(2)}, u32[]{:S(2)}) collective-permute-start(bf16[320,128]{1,0:T(8,128)(2,1)S(1)} %pad_maximum_fusion), channel_id=1, source_target_pairs={{0,12},{2,14},{4,8},{6,10},{8,4},{10,6},{12,0},{14,2},{1,13},{3,15... | collective-permute-start | bytes 245768 | tf_op jit(solution)/shard_map/ppermute | solution.py:267
  38.1 0.1 collective-permute-done.12.refs_2_
  38.2 2.9 %collective-permute-done.10.refs_1_ = bf16[320,128]{1,0:T(8,128)(2,1)S(1)} collective-permute-done((bf16[320,128]{1,0:T(8,128)(2,1)S(1)}, bf16[320,128]{1,0:T(8,128)(2,1)S(1)}, u32[]{:S(2)}, u32[]{:S(2)}) %collective-permute-start.10) | collective-permute-done | bytes 81952 | tf_op jit(solution)/shard_map/ppermute | solution.py:267
  41.1 1.6 %collective-permute-done.8.refs_0_ = bf16[320,128]{1,0:T(8,128)(2,1)S(1)} collective-permute-done((bf16[320,128]{1,0:T(8,128)(2,1)S(1)}, bf16[320,128]{1,0:T(8,128)(2,1)S(1)}, u32[]{:S(2)}, u32[]{:S(2)}) %collective-permute-start.8) | collective-permute-done | bytes 81952 | tf_op jit(solution)/shard_map/ppermute | solution.py:267
  42.7 0.7 %shard_map.66 = f32[4,8192]{1,0:T(4,128)} custom-call(f32[256,128]{1,0:T(8,128)S(1)} %get-tuple-element.20.scale_ref, bf16[320,128]{1,0:T(8,128)(2,1)S(1)} %collective-permute-done.8.refs_0_, bf16[320,128]{1,0:T(8,128)(2,1)S(1)} %collective-permute-done.10.refs_1_, bf16[320,128]{1,0:T(8,128)(2,1)S(1)} %collective-permute-done.12.refs_2_, ...), custom_call_target="tpu_custom_call" | custom-call | tf_op jit(solution)/shard_map/pallas_call | solution.py:228
  (30 shorter events, 0.3 us)
Async XLA Ops:
  1.1 7.4 %collective-permute-start.1 = (bf16[384,128]{1,0:T(8,128)(2,1)S(1)}, bf16[384,128]{1,0:T(8,128)(2,1)S(1)}, u32[]{:S(2)}, u32[]{:S(2)}) collective-permute-start(bf16[384,128]{1,0:T(8,128)(2,1)S(1)} %get-tuple-element.24), channel_id=1, source_target_pairs={{0,4},{2,6},{4,0},{6,2},{8,12},{10,14},{12,8},{14,10},{1,5},{3,7},... | collective-permute-start | bytes 294920 | tf_op jit(solution)/shard_map/ppermute | solution.py:267
  4.2 10.4 %collective-permute-start.3 = (bf16[384,128]{1,0:T(8,128)(2,1)S(1)}, bf16[384,128]{1,0:T(8,128)(2,1)S(1)}, u32[]{:S(2)}, u32[]{:S(2)}) collective-permute-start(bf16[384,128]{1,0:T(8,128)(2,1)S(1)} %get-tuple-element.25), channel_id=1, source_target_pairs={{0,8},{2,10},{4,12},{6,14},{8,0},{10,2},{12,4},{14,6},{1,9},{3,11}... | collective-permute-start | bytes 294920 | tf_op jit(solution)/shard_map/ppermute | solution.py:267
  6.8 9.4 %collective-permute-start.5 = (bf16[384,128]{1,0:T(8,128)(2,1)S(1)}, bf16[384,128]{1,0:T(8,128)(2,1)S(1)}, u32[]{:S(2)}, u32[]{:S(2)}) collective-permute-start(bf16[384,128]{1,0:T(8,128)(2,1)S(1)} %get-tuple-element.26), channel_id=1, source_target_pairs={{0,12},{2,14},{4,8},{6,10},{8,4},{10,6},{12,0},{14,2},{1,13},{3,15... | collective-permute-start | bytes 294920 | tf_op jit(solution)/shard_map/ppermute | solution.py:267
  6.8 9.9 %collective-permute-start = (bf16[320,128]{1,0:T(8,128)(2,1)S(1)}, bf16[320,128]{1,0:T(8,128)(2,1)S(1)}, u32[]{:S(2)}, u32[]{:S(2)}) collective-permute-start(bf16[320,128]{1,0:T(8,128)(2,1)S(1)} %get-tuple-element.23), channel_id=1, source_target_pairs={{0,2},{2,0},{4,6},{6,4},{8,10},{10,8},{12,14},{14,12},{1,3},{3,1},... | collective-permute-start | bytes 245768 | tf_op jit(solution)/shard_map/ppermute | solution.py:267
  8.5 8.2 %collective-permute-start.2 = (bf16[320,128]{1,0:T(8,128)(2,1)S(1)}, bf16[320,128]{1,0:T(8,128)(2,1)S(1)}, u32[]{:S(2)}, u32[]{:S(2)}) collective-permute-start(bf16[320,128]{1,0:T(8,128)(2,1)S(1)} %slice.76), channel_id=1, source_target_pairs={{0,2},{2,0},{4,6},{6,4},{8,10},{10,8},{12,14},{14,12},{1,3},{3,1},... | collective-permute-start | bytes 245768 | tf_op jit(solution)/shard_map/ppermute | solution.py:267
  14.6 4.4 %collective-permute-start.4 = (bf16[320,128]{1,0:T(8,128)(2,1)S(1)}, bf16[320,128]{1,0:T(8,128)(2,1)S(1)}, u32[]{:S(2)}, u32[]{:S(2)}) collective-permute-start(bf16[320,128]{1,0:T(8,128)(2,1)S(1)} %slice.77), channel_id=1, source_target_pairs={{0,2},{2,0},{4,6},{6,4},{8,10},{10,8},{12,14},{14,12},{1,3},{3,1},... | collective-permute-start | bytes 245768 | tf_op jit(solution)/shard_map/ppermute | solution.py:267
  16.2 4.5 %collective-permute-start.6 = (bf16[320,128]{1,0:T(8,128)(2,1)S(1)}, bf16[320,128]{1,0:T(8,128)(2,1)S(1)}, u32[]{:S(2)}, u32[]{:S(2)}) collective-permute-start(bf16[320,128]{1,0:T(8,128)(2,1)S(1)} %slice.78), channel_id=1, source_target_pairs={{0,2},{2,0},{4,6},{6,4},{8,10},{10,8},{12,14},{14,12},{1,3},{3,1},... | collective-permute-start | bytes 245768 | tf_op jit(solution)/shard_map/ppermute | solution.py:267
  28.3 4.4 %collective-permute-start.11 = (bf16[288,128]{1,0:T(8,128)(2,1)S(1)}, bf16[288,128]{1,0:T(8,128)(2,1)S(1)}, u32[]{:S(2)}, u32[]{:S(2)}) collective-permute-start(bf16[288,128]{1,0:T(8,128)(2,1)S(1)} %get-tuple-element.32), channel_id=1, source_target_pairs={{0,2},{2,0},{4,6},{6,4},{8,10},{10,8},{12,14},{14,12},{1,3},{3,1},... | collective-permute-start | bytes 221192 | tf_op jit(solution)/shard_map/ppermute | solution.py:267
  29.1 7.0 %collective-permute-start.13 = (bf16[288,128]{1,0:T(8,128)(2,1)S(1)}, bf16[288,128]{1,0:T(8,128)(2,1)S(1)}, u32[]{:S(2)}, u32[]{:S(2)}) collective-permute-start(bf16[288,128]{1,0:T(8,128)(2,1)S(1)} %get-tuple-element.34), channel_id=1, source_target_pairs={{0,2},{2,0},{4,6},{6,4},{8,10},{10,8},{12,14},{14,12},{1,3},{3,1},... | collective-permute-start | bytes 221192 | tf_op jit(solution)/shard_map/ppermute | solution.py:267
  30.4 4.4 %collective-permute-start.9 = (bf16[288,128]{1,0:T(8,128)(2,1)S(1)}, bf16[288,128]{1,0:T(8,128)(2,1)S(1)}, u32[]{:S(2)}, u32[]{:S(2)}) collective-permute-start(bf16[288,128]{1,0:T(8,128)(2,1)S(1)} %get-tuple-element.30), channel_id=1, source_target_pairs={{0,2},{2,0},{4,6},{6,4},{8,10},{10,8},{12,14},{14,12},{1,3},{3,1},... | collective-permute-start | bytes 221192 | tf_op jit(solution)/shard_map/ppermute | solution.py:267
  31.1 5.1 %collective-permute-start.7 = (bf16[288,128]{1,0:T(8,128)(2,1)S(1)}, bf16[288,128]{1,0:T(8,128)(2,1)S(1)}, u32[]{:S(2)}, u32[]{:S(2)}) collective-permute-start(bf16[288,128]{1,0:T(8,128)(2,1)S(1)} %get-tuple-element.28), channel_id=1, source_target_pairs={{0,2},{2,0},{4,6},{6,4},{8,10},{10,8},{12,14},{14,12},{1,3},{3,1},... | collective-permute-start | bytes 221192 | tf_op jit(solution)/shard_map/ppermute | solution.py:267
  32.8 5.4 %collective-permute-start.12 = (bf16[320,128]{1,0:T(8,128)(2,1)S(1)}, bf16[320,128]{1,0:T(8,128)(2,1)S(1)}, u32[]{:S(2)}, u32[]{:S(2)}) collective-permute-start(bf16[320,128]{1,0:T(8,128)(2,1)S(1)} %pad_maximum_fusion.2), channel_id=1, source_target_pairs={{0,4},{2,6},{4,0},{6,2},{8,12},{10,14},{12,8},{14,10},{1,5},{3,7},... | collective-permute-start | bytes 245768 | tf_op jit(solution)/shard_map/ppermute | solution.py:267
  34.8 6.3 %collective-permute-start.10 = (bf16[320,128]{1,0:T(8,128)(2,1)S(1)}, bf16[320,128]{1,0:T(8,128)(2,1)S(1)}, u32[]{:S(2)}, u32[]{:S(2)}) collective-permute-start(bf16[320,128]{1,0:T(8,128)(2,1)S(1)} %pad_maximum_fusion.1), channel_id=1, source_target_pairs={{0,8},{2,10},{4,12},{6,14},{8,0},{10,2},{12,4},{14,6},{1,9},{3,11}... | collective-permute-start | bytes 245768 | tf_op jit(solution)/shard_map/ppermute | solution.py:267
  36.3 6.4 %collective-permute-start.8 = (bf16[320,128]{1,0:T(8,128)(2,1)S(1)}, bf16[320,128]{1,0:T(8,128)(2,1)S(1)}, u32[]{:S(2)}, u32[]{:S(2)}) collective-permute-start(bf16[320,128]{1,0:T(8,128)(2,1)S(1)} %pad_maximum_fusion), channel_id=1, source_target_pairs={{0,12},{2,14},{4,8},{6,10},{8,4},{10,6},{12,0},{14,2},{1,13},{3,15... | collective-permute-start | bytes 245768 | tf_op jit(solution)/shard_map/ppermute | solution.py:267

commit v3 on v2

--- a/solution.py
+++ b/solution.py
@@ -93,18 +93,52 @@
     )(*held)
 
 
-def adjoint_kernel(peers, rows, epochs, group, table_ref, *refs):
-    piece_refs, tiles_ref = refs[:peers], refs[peers]
-    out_refs = refs[peers + 1 : 2 * peers + 1]
-    tiles, emission, loss, collected, sems = refs[2 * peers + 1 :]
+def load_kernel(after_ref, tiles_ref, out_ref, sems):
+    loads = [
+        pltpu.make_async_copy(tiles_ref.at[r], out_ref.at[r], sems.at[r])
+        for r in range(out_ref.shape[0])
+    ]
+    for load in loads:
+        load.start()
+    for load in loads:
+        load.wait()
+
+
+def load_tiles(tiles, after, rows):
+    return pl.pallas_call(
+        load_kernel,
+        in_specs=[pl.BlockSpec(memory_space=pl.ANY)] * 2,
+        out_specs=RESIDENT,
+        scratch_shapes=[pltpu.SemaphoreType.DMA((rows,))],
+        out_shape=jax.ShapeDtypeStruct((rows, *tiles.shape[1:]), tiles.dtype),
+        compiler_params=pltpu.CompilerParams(vmem_limit_bytes=2 * tiles.size + (1 << 20)),
+        cost_estimate=pl.CostEstimate(
+            flops=0, bytes_accessed=4 * tiles.size, transcendentals=0
+        ),
+    )(after, tiles)
+
+
+def adjoint_kernel(order, rows, epochs, group, table_ref, *refs):
+    peers = len(order)
+    piece_refs = [refs[order.index(p)] for p in range(peers)]
+    early_ref, tiles_ref = refs[peers : peers + 2]
+    out_refs = refs[peers + 2 : 2 * peers + 2]
+    late_ref, emission, loss, collected, sems = refs[2 * peers + 2 :]
     blocks_all, samples, side = emission.shape[0] - 1, emission.shape[1], emission.shape[2]
-    slots = tiles.shape[1]
+    early, slots = early_ref.shape[:2]
+    loads = [
+        pltpu.make_async_copy(tiles_ref.at[early + r], late_ref.at[r], sems.at[r])
+        for r in range(rows - early)
+    ]
+    for load in loads:
+        load.start()
+
+    def stored_tiles(r, span):
+        ref, r = (early_ref, r) if r < early else (late_ref, r - early)
+        return jnp.concatenate([ref[r, k] for k in span], 1)
+
     part, wide = rows * epochs, blocks_all * epochs
     me = lax.axis_index("node")
-
-    loads = [pltpu.make_async_copy(tiles_ref.at[r], tiles.at[r], sems.at[r]) for r in range(rows)]
-    for load in loads:
-        load.start()
 
     emit_at = [2 * part if p and not p & 1 else 0 for p in range(peers)]
     loss_at = [0 if p and not p & 1 else wide for p in range(peers)]
@@ -135,29 +169,36 @@
     emission[blocks_all] = jnp.zeros(emission.shape[1:], BF16)
     collected[...] = jnp.zeros_like(collected)
 
-    for block_rows in [range(first, first + 4) for first in range(0, rows, 4)]:
+    def find_weight(r):
+        flux = jnp.zeros((samples, side), F32)
+        for first in range(0, slots, group):
+            span = range(first, first + group)
+            picked = jnp.concatenate([emission[table_ref[r, k]] for k in span], 1)
+            stored = stored_tiles(r, span)
+            part = lax.dot_general(
+                stored, picked, (((1,), (1,)), ((), ())), preferred_element_type=F32
+            )
+            flux = part if first == 0 else flux + part
+        flux = flux.T
+        own = me * rows + r
+        weight = loss[r] * (flux - emission[own].astype(F32))
+        collected[own] -= weight
+        return weight.astype(BF16)
+
+    def add_terms(r, weight):
+        for first in range(0, slots, group):
+            stored = stored_tiles(r, range(first, first + group))
+            terms = jnp.dot(weight, stored, preferred_element_type=F32)
+            for k in range(group):
+                collected[table_ref[r, first + k]] += terms[:, k * side : (k + 1) * side]
+
+    for block_rows in (range(early), range(early, rows)):
         for r in block_rows:
-            loads[r].wait()
-        weights = {}
-        for r in block_rows:
-            flux = jnp.zeros((samples, side), F32)
-            for first in range(0, slots, group):
-                span = range(first, first + group)
-                picked = jnp.concatenate([emission[table_ref[r, k]] for k in span], 1)
-                stored = jnp.concatenate([tiles[r, k] for k in span], 1)
-                flux += lax.dot_general(
-                    picked, stored, (((1,), (1,)), ((), ())), preferred_element_type=F32
-                )
-            own = me * rows + r
-            weight = loss[r] * (flux - emission[own].astype(F32))
-            weights[r] = weight.astype(BF16)
-            collected[own] -= weight
-        for r in block_rows:
-            for first in range(0, slots, group):
-                stored = jnp.concatenate([tiles[r, k] for k in range(first, first + group)], 1)
-                terms = jnp.dot(weights[r], stored, preferred_element_type=F32)
-                for k in range(group):
-                    collected[table_ref[r, first + k]] += terms[:, k * side : (k + 1) * side]
+            if r >= early:
+                loads[r - early].wait()
+        weights = [find_weight(r) for r in block_rows]
+        for r, weight in zip(block_rows, weights):
+            add_terms(r, weight)
 
     @pl.loop(0, blocks_all // 4)
     def _(quad):
@@ -175,29 +216,29 @@
             ref[wide + first * epochs : wide + (first + 4) * epochs, :] = halves(full)[1]
 
 
-def adjoint_terms(table, pieces, tiles, epochs, blocks_all):
+def adjoint_terms(table, order, pieces, early, tiles, epochs, blocks_all):
     peers = len(pieces)
     rows, slots, side = tiles.shape[:3]
     samples = peers * epochs
     out_rows = (blocks_all + rows) * epochs
     need = (
         (blocks_all + 1) * samples * side * 6
+        + rows * slots * side * side * 2
         + 2 * peers * out_rows * side * 2
-        + rows * slots * side * side * 2
         + rows * samples * side * 4
     )
     return pl.pallas_call(
-        functools.partial(adjoint_kernel, peers, rows, epochs, min(8, slots)),
+        functools.partial(adjoint_kernel, order, rows, epochs, min(8, slots)),
         in_specs=[pl.BlockSpec(memory_space=pltpu.SMEM)]
-        + [RESIDENT] * peers
+        + [RESIDENT] * (peers + 1)
         + [pl.BlockSpec(memory_space=pl.ANY)],
         out_specs=[RESIDENT] * peers,
         scratch_shapes=[
-            pltpu.VMEM(tiles.shape, BF16),
+            pltpu.VMEM((rows - early.shape[0], *tiles.shape[1:]), BF16),
             pltpu.VMEM((blocks_all + 1, samples, side), BF16),
             pltpu.VMEM((rows, samples, side), F32),
             pltpu.VMEM((blocks_all + 1, samples, side), F32),
-            pltpu.SemaphoreType.DMA((rows,)),
+            pltpu.SemaphoreType.DMA((rows - early.shape[0],)),
         ],
         out_shape=[jax.ShapeDtypeStruct((out_rows, side), BF16)] * peers,
         compiler_params=pltpu.CompilerParams(vmem_limit_bytes=need + (6 << 20)),
@@ -206,7 +247,7 @@
             bytes_accessed=rows * slots * side * side * 2,
             transcendentals=0,
         ),
-    )(table, *pieces, pltpu.with_memory_space_constraint(tiles, pltpu.HBM))
+    )(table, *[pieces[p] for p in order], early, tiles)
 
 
 def finish_kernel(steps, rows, epochs, scale_ref, *refs):
@@ -243,9 +284,10 @@
         [jnp.where(odd, low_theirs, low_mine), jnp.where(odd, low_mine, low_theirs)], 0
     )
     start = (me // 2) * low.shape[0]
-    high, low = halves(lax.dynamic_slice_in_dim(total, start, low.shape[0], 0) + low)
-    total = lax.dynamic_update_slice_in_dim(total.astype(BF16), high, start, 0)
-    return jnp.concatenate([total, low], 0)
+    window = lax.dynamic_slice_in_dim(total, start, low.shape[0], 0) + low
+    high = lax.reduce_precision(window, 8, 7)
+    total = lax.dynamic_update_slice_in_dim(total.astype(BF16), high.astype(BF16), start, 0)
+    return jnp.concatenate([total, (window - high).astype(BF16)], 0)
 
 
 def on_device(
@@ -283,14 +325,16 @@
     for p in far:
         pieces[p ^ 1] = send(pieces[p][2 * rows * epochs :], 1)
 
-    terms = adjoint_terms(
-        table, [pieces[p] for p in range(nodes)], gebhart_tiles, epochs, blocks_all
-    )
-
-    steps = (*far, 0)
+    near = [nodes // 2 - 1, *([1] if nodes > 4 else []), *range(nodes // 2 - 2, 1, -1), 0]
+    order = tuple(q for d in near for q in (2 * d + 1, 2 * d))
+    tiles = pltpu.with_memory_space_constraint(gebhart_tiles, pltpu.HBM)
+    early = load_tiles(tiles, pieces[far[0]], rows // 2)
+    terms = adjoint_terms(table, order, pieces, early, tiles, epochs, blocks_all)
+
+    steps = tuple(range(0, nodes, 2))
     arrived = {p: send(terms[p ^ 1], 1) for p in steps}
     paired = {p: add_neighbour(me, wide, terms[p], arrived[p]) for p in steps}
-    sums = [send(paired[p], p) for p in far] + [paired[0]]
+    sums = [paired[0]] + [send(paired[p], p) for p in steps[1:]]
     return finish(steps, rows, epochs, scale, sums)
 
 

time: 43.7 us -> 38.7 us (0.89)
  waiting for transfers between devices: 15.6 us -> 7.99 us
  starting transfers between devices: 17.9 us -> 20.9 us
    ppermute x14, waiting for transfers between devices: 15.6 us -> 7.99 us  [send(): return lax.ppermute(value, 'node', [(i, i ^ step) for i in range(nodes)])]
    ppermute x14, starting transfers between devices: 17.9 us -> 20.9 us  [send(): return lax.ppermute(value, 'node', [(i, i ^ step) for i in range(nodes)])]
    pallas_call x1 -> x2, Pallas kernels: 7.6 us -> 7.3 us  [the longest x1 5.1 us: adjoint_terms(): pl.pallas_call(functools.partial(adjoint_kernel, order, rows, epochs, min...]
  transfers between devices with their start and end apart: 14 -> 14, of which waited for: 8 -> 8; matrix products, arithmetic and copies ran while one was open for 1% -> 1% of each run, Pallas kernels for 0% -> 6%
where the time goes in v3:
time: 38.7 us; the launch traced here: 38.5 us
  starting transfers between devices  20.9 us (54%)
  Pallas kernels  9.13 us (24%)
  waiting for transfers between devices  7.99 us (21%)
    ppermute x14, starting transfers between devices, send(): return lax.ppermute(value, 'node', [(i, i ^ step) for i in range(nodes)])  20.9 us
    ppermute x14, waiting for transfers between devices, send(): return lax.ppermute(value, 'node', [(i, i ^ step) for i in range(nodes)])  7.99 us
    pallas_call x1, Pallas kernels, adjoint_terms(): pl.pallas_call(functools.partial(adjoint_kernel, order, rows, epochs, min...  5.1 us
    pallas_call x1, Pallas kernels, load_tiles(): pl.pallas_call(load_kernel, in_specs=[pl.BlockSpec(memory_space=pl.ANY)]...  2.2 us
    pallas_call x1, Pallas kernels, prepare(): pl.pallas_call(functools.partial(prepare_kernel, far, rows), grid=(1,), i...  1.09 us
  transfers between devices with their start and end apart: 14, of which 8 were waited for; matrix products, arithmetic and copies ran while one was open for 1% of the time, Pallas kernels for 6%

profile of v3, /device:TPU:0, one launch (start us, length us, event | category | flops | bytes accessed | tf_op | source)
XLA Modules:
  0.0 38.5 jit_solution(3811238819431295788)
XLA Ops:
  0.0 1.1 %shard_map.64 = (bf16[384,128]{1,0:T(8,128)(2,1)S(1)}, bf16[384,128]{1,0:T(8,128)(2,1)S(1)}, bf16[384,128]{1,0:T(8,128)(2,1)S(1)}, bf16[320,128]{1,0:T(8,128)(2,...) custom-call(f32[4,8192]{1,0:T(4,128)} %kelvin_ref.1, f32[64,128]{1,0:T(8,128)} %bitcast.1, ...), custom_call_target="tpu_custom_call" | custom-call | tf_op jit(solution)/shard_map/pallas_call | solution.py:84
  1.1 5.1 %collective-permute-start = (bf16[384,128]{1,0:T(8,128)(2,1)S(1)}, bf16[384,128]{1,0:T(8,128)(2,1)S(1)}, u32[]{:S(2)}, u32[]{:S(2)}) collective-permute-start(bf16[384,128]{1,0:T(8,128)(2,1)S(1)} %get-tuple-element.22), channel_id=1, source_target_pairs={{0,12},{2,14},{4,8},{6,10},{8,4},{10,6},{12,0},{14,2},{1,13},{3,15... | collective-permute-start | bytes 294920 | tf_op jit(solution)/shard_map/ppermute | solution.py:309
  6.2 0.6 %collective-permute-start.4 = (bf16[384,128]{1,0:T(8,128)(2,1)S(1)}, bf16[384,128]{1,0:T(8,128)(2,1)S(1)}, u32[]{:S(2)}, u32[]{:S(2)}) collective-permute-start(bf16[384,128]{1,0:T(8,128)(2,1)S(1)} %get-tuple-element.24), channel_id=1, source_target_pairs={{0,8},{2,10},{4,12},{6,14},{8,0},{10,2},{12,4},{14,6},{1,9},{3,11}... | collective-permute-start | bytes 294920 | tf_op jit(solution)/shard_map/ppermute | solution.py:309
  6.9 1.7 %collective-permute-start.6 = (bf16[320,128]{1,0:T(8,128)(2,1)S(1)}, bf16[320,128]{1,0:T(8,128)(2,1)S(1)}, u32[]{:S(2)}, u32[]{:S(2)}) collective-permute-start(bf16[320,128]{1,0:T(8,128)(2,1)S(1)} %get-tuple-element.25), channel_id=1, source_target_pairs={{0,2},{2,0},{4,6},{6,4},{8,10},{10,8},{12,14},{14,12},{1,3},{3,1},... | collective-permute-start | bytes 245768 | tf_op jit(solution)/shard_map/ppermute | solution.py:309
  8.5 1.4 %collective-permute-done.after_ref.refs_1_ = bf16[384,128]{1,0:T(8,128)(2,1)S(1)} collective-permute-done((bf16[384,128]{1,0:T(8,128)(2,1)S(1)}, bf16[384,128]{1,0:T(8,128)(2,1)S(1)}, u32[]{:S(2)}, u32[]{:S(2)}) %collective-permute-start) | collective-permute-done | bytes 98336 | tf_op jit(solution)/shard_map/ppermute | solution.py:309
  9.9 1.7 %collective-permute-start.1 = (bf16[320,128]{1,0:T(8,128)(2,1)S(1)}, bf16[320,128]{1,0:T(8,128)(2,1)S(1)}, u32[]{:S(2)}, u32[]{:S(2)}) collective-permute-start(bf16[320,128]{1,0:T(8,128)(2,1)S(1)} %slice.76), channel_id=1, source_target_pairs={{0,2},{2,0},{4,6},{6,4},{8,10},{10,8},{12,14},{14,12},{1,3},{3,1},... | collective-permute-start | bytes 245768 | tf_op jit(solution)/shard_map/ppermute | solution.py:309
  11.6 0.6 %collective-permute-done.2.refs_3_ = bf16[384,128]{1,0:T(8,128)(2,1)S(1)} collective-permute-done((bf16[384,128]{1,0:T(8,128)(2,1)S(1)}, bf16[384,128]{1,0:T(8,128)(2,1)S(1)}, u32[]{:S(2)}, u32[]{:S(2)}) %collective-permute-start.2) | collective-permute-done | bytes 98336 | tf_op jit(solution)/shard_map/ppermute | solution.py:309
  12.2 1.5 %collective-permute-start.3 = (bf16[320,128]{1,0:T(8,128)(2,1)S(1)}, bf16[320,128]{1,0:T(8,128)(2,1)S(1)}, u32[]{:S(2)}, u32[]{:S(2)}) collective-permute-start(bf16[320,128]{1,0:T(8,128)(2,1)S(1)} %slice.77), channel_id=1, source_target_pairs={{0,2},{2,0},{4,6},{6,4},{8,10},{10,8},{12,14},{14,12},{1,3},{3,1},... | collective-permute-start | bytes 245768 | tf_op jit(solution)/shard_map/ppermute | solution.py:309
  13.8 0.7 %collective-permute-done.4.refs_5_ = bf16[384,128]{1,0:T(8,128)(2,1)S(1)} collective-permute-done((bf16[384,128]{1,0:T(8,128)(2,1)S(1)}, bf16[384,128]{1,0:T(8,128)(2,1)S(1)}, u32[]{:S(2)}, u32[]{:S(2)}) %collective-permute-start.4) | collective-permute-done | bytes 98336 | tf_op jit(solution)/shard_map/ppermute | solution.py:309
  14.5 1.5 %collective-permute-start.5 = (bf16[320,128]{1,0:T(8,128)(2,1)S(1)}, bf16[320,128]{1,0:T(8,128)(2,1)S(1)}, u32[]{:S(2)}, u32[]{:S(2)}) collective-permute-start(bf16[320,128]{1,0:T(8,128)(2,1)S(1)} %slice.78), channel_id=1, source_target_pairs={{0,2},{2,0},{4,6},{6,4},{8,10},{10,8},{12,14},{14,12},{1,3},{3,1},... | collective-permute-start | bytes 245768 | tf_op jit(solution)/shard_map/ppermute | solution.py:309
  16.0 2.2 %shard_map.65.refs_8_ = bf16[4,32,128,128]{3,2,1,0:T(8,128)(2,1)S(1)} custom-call(bf16[384,128]{1,0:T(8,128)(2,1)S(1)} %collective-permute-done.after_ref.refs_1_, bf16[8,32,128,128]{3,2,1,0:T(8,128)(2,1)} %refs_9_.1), custom_call_target="tpu_custom_call" | custom-call | bytes 16777216 | tf_op jit(solution)/shard_map/pallas_call | solution.py:108
  18.3 0.7 %collective-permute-done.5.refs_4_ = bf16[320,128]{1,0:T(8,128)(2,1)S(1)} collective-permute-done((bf16[320,128]{1,0:T(8,128)(2,1)S(1)}, bf16[320,128]{1,0:T(8,128)(2,1)S(1)}, u32[]{:S(2)}, u32[]{:S(2)}) %collective-permute-start.5) | collective-permute-done | bytes 81952 | tf_op jit(solution)/shard_map/ppermute | solution.py:309
  18.9 5.1 %shard_map.66 = (bf16[288,128]{1,0:T(8,128)(2,1)S(1)}, bf16[288,128]{1,0:T(8,128)(2,1)S(1)}, bf16[288,128]{1,0:T(8,128)(2,1)S(1)}, bf16[288,128]{1,0:T(8,128)(2,...) custom-call(s32[8,32]{1,0:T(8,128)S(1)} %get-tuple-element.21.table_, ...), custom_call_target="tpu_custom_call" | custom-call | flops 536870912 | bytes 8388608 | tf_op jit(solution)/shard_map/pallas_call | solution.py:230
  24.0 1.6 %collective-permute-start.12 = (bf16[288,128]{1,0:T(8,128)(2,1)S(1)}, bf16[288,128]{1,0:T(8,128)(2,1)S(1)}, u32[]{:S(2)}, u32[]{:S(2)}) collective-permute-start(bf16[288,128]{1,0:T(8,128)(2,1)S(1)} %get-tuple-element.34), channel_id=1, source_target_pairs={{0,2},{2,0},{4,6},{6,4},{8,10},{10,8},{12,14},{14,12},{1,3},{3,1},... | collective-permute-start | bytes 221192 | tf_op jit(solution)/shard_map/ppermute | solution.py:309
  25.7 0.5 %collective-permute-start.10 = (bf16[288,128]{1,0:T(8,128)(2,1)S(1)}, bf16[288,128]{1,0:T(8,128)(2,1)S(1)}, u32[]{:S(2)}, u32[]{:S(2)}) collective-permute-start(bf16[288,128]{1,0:T(8,128)(2,1)S(1)} %get-tuple-element.32), channel_id=1, source_target_pairs={{0,2},{2,0},{4,6},{6,4},{8,10},{10,8},{12,14},{14,12},{1,3},{3,1},... | collective-permute-start | bytes 221192 | tf_op jit(solution)/shard_map/ppermute | solution.py:309
  26.1 1.6 %collective-permute-start.8 = (bf16[288,128]{1,0:T(8,128)(2,1)S(1)}, bf16[288,128]{1,0:T(8,128)(2,1)S(1)}, u32[]{:S(2)}, u32[]{:S(2)}) collective-permute-start(bf16[288,128]{1,0:T(8,128)(2,1)S(1)} %get-tuple-element.30), channel_id=1, source_target_pairs={{0,2},{2,0},{4,6},{6,4},{8,10},{10,8},{12,14},{14,12},{1,3},{3,1},... | collective-permute-start | bytes 221192 | tf_op jit(solution)/shard_map/ppermute | solution.py:309
  27.7 0.5 %collective-permute-start.7 = (bf16[288,128]{1,0:T(8,128)(2,1)S(1)}, bf16[288,128]{1,0:T(8,128)(2,1)S(1)}, u32[]{:S(2)}, u32[]{:S(2)}) collective-permute-start(bf16[288,128]{1,0:T(8,128)(2,1)S(1)} %get-tuple-element.28), channel_id=1, source_target_pairs={{0,2},{2,0},{4,6},{6,4},{8,10},{10,8},{12,14},{14,12},{1,3},{3,1},... | collective-permute-start | bytes 221192 | tf_op jit(solution)/shard_map/ppermute | solution.py:309
  28.2 1.1 %collective-permute-done.12 = bf16[288,128]{1,0:T(8,128)(2,1)S(1)} collective-permute-done((bf16[288,128]{1,0:T(8,128)(2,1)S(1)}, bf16[288,128]{1,0:T(8,128)(2,1)S(1)}, u32[]{:S(2)}, u32[]{:S(2)}) %collective-permute-start.12) | collective-permute-done | bytes 73760 | tf_op jit(solution)/shard_map/ppermute | solution.py:309
  29.4 2.7 %collective-permute-start.13 = (bf16[320,128]{1,0:T(8,128)(2,1)S(1)}, bf16[320,128]{1,0:T(8,128)(2,1)S(1)}, u32[]{:S(2)}, u32[]{:S(2)}) collective-permute-start(bf16[320,128]{1,0:T(8,128)(2,1)S(1)} %pad_maximum_fusion.3), channel_id=1, source_target_pairs={{0,12},{2,14},{4,8},{6,10},{8,4},{10,6},{12,0},{14,2},{1,13},{3,15... | collective-permute-start | bytes 245768 | tf_op jit(solution)/shard_map/ppermute | solution.py:309
  32.2 0.1 collective-permute-start.11
  32.4 1.8 %collective-permute-start.9 = (bf16[320,128]{1,0:T(8,128)(2,1)S(1)}, bf16[320,128]{1,0:T(8,128)(2,1)S(1)}, u32[]{:S(2)}, u32[]{:S(2)}) collective-permute-start(bf16[320,128]{1,0:T(8,128)(2,1)S(1)} %pad_maximum_fusion.1), channel_id=1, source_target_pairs={{0,4},{2,6},{4,0},{6,2},{8,12},{10,14},{12,8},{14,10},{1,5},{3,7},... | collective-permute-start | bytes 245768 | tf_op jit(solution)/shard_map/ppermute | solution.py:309
  34.3 1.5 %collective-permute-done.13.refs_3_ = bf16[320,128]{1,0:T(8,128)(2,1)S(1)} collective-permute-done((bf16[320,128]{1,0:T(8,128)(2,1)S(1)}, bf16[320,128]{1,0:T(8,128)(2,1)S(1)}, u32[]{:S(2)}, u32[]{:S(2)}) %collective-permute-start.13) | collective-permute-done | bytes 81952 | tf_op jit(solution)/shard_map/ppermute | solution.py:309
  35.8 1.9 %collective-permute-done.11.refs_2_ = bf16[320,128]{1,0:T(8,128)(2,1)S(1)} collective-permute-done((bf16[320,128]{1,0:T(8,128)(2,1)S(1)}, bf16[320,128]{1,0:T(8,128)(2,1)S(1)}, u32[]{:S(2)}, u32[]{:S(2)}) %collective-permute-start.11) | collective-permute-done | bytes 81952 | tf_op jit(solution)/shard_map/ppermute | solution.py:309
  37.8 0.7 %shard_map.67 = f32[4,8192]{1,0:T(4,128)} custom-call(f32[256,128]{1,0:T(8,128)S(1)} %get-tuple-element.20.scale_ref, bf16[320,128]{1,0:T(8,128)(2,1)S(1)} %pad_maximum_fusion.refs_0_, bf16[320,128]{1,0:T(8,128)(2,1)S(1)} %collective-permute-done.9.refs_1_, bf16[320,128]{1,0:T(8,128)(2,1)S(1)} %collective-permute-done.11.refs_2_, ...), custom_call_target="tpu_custom_call" | custom-call | tf_op jit(solution)/shard_map/pallas_call | solution.py:269
  (31 shorter events, 0.4 us)
Async XLA Ops:
  1.1 8.8 %collective-permute-start = (bf16[384,128]{1,0:T(8,128)(2,1)S(1)}, bf16[384,128]{1,0:T(8,128)(2,1)S(1)}, u32[]{:S(2)}, u32[]{:S(2)}) collective-permute-start(bf16[384,128]{1,0:T(8,128)(2,1)S(1)} %get-tuple-element.22), channel_id=1, source_target_pairs={{0,12},{2,14},{4,8},{6,10},{8,4},{10,6},{12,0},{14,2},{1,13},{3,15... | collective-permute-start | bytes 294920 | tf_op jit(solution)/shard_map/ppermute | solution.py:309
  6.2 6.0 %collective-permute-start.2 = (bf16[384,128]{1,0:T(8,128)(2,1)S(1)}, bf16[384,128]{1,0:T(8,128)(2,1)S(1)}, u32[]{:S(2)}, u32[]{:S(2)}) collective-permute-start(bf16[384,128]{1,0:T(8,128)(2,1)S(1)} %get-tuple-element.23), channel_id=1, source_target_pairs={{0,4},{2,6},{4,0},{6,2},{8,12},{10,14},{12,8},{14,10},{1,5},{3,7},... | collective-permute-start | bytes 294920 | tf_op jit(solution)/shard_map/ppermute | solution.py:309
  6.2 8.3 %collective-permute-start.4 = (bf16[384,128]{1,0:T(8,128)(2,1)S(1)}, bf16[384,128]{1,0:T(8,128)(2,1)S(1)}, u32[]{:S(2)}, u32[]{:S(2)}) collective-permute-start(bf16[384,128]{1,0:T(8,128)(2,1)S(1)} %get-tuple-element.24), channel_id=1, source_target_pairs={{0,8},{2,10},{4,12},{6,14},{8,0},{10,2},{12,4},{14,6},{1,9},{3,11}... | collective-permute-start | bytes 294920 | tf_op jit(solution)/shard_map/ppermute | solution.py:309
  6.9 11.4 %collective-permute-start.6 = (bf16[320,128]{1,0:T(8,128)(2,1)S(1)}, bf16[320,128]{1,0:T(8,128)(2,1)S(1)}, u32[]{:S(2)}, u32[]{:S(2)}) collective-permute-start(bf16[320,128]{1,0:T(8,128)(2,1)S(1)} %get-tuple-element.25), channel_id=1, source_target_pairs={{0,2},{2,0},{4,6},{6,4},{8,10},{10,8},{12,14},{14,12},{1,3},{3,1},... | collective-permute-start | bytes 245768 | tf_op jit(solution)/shard_map/ppermute | solution.py:309
  9.9 8.3 %collective-permute-start.1 = (bf16[320,128]{1,0:T(8,128)(2,1)S(1)}, bf16[320,128]{1,0:T(8,128)(2,1)S(1)}, u32[]{:S(2)}, u32[]{:S(2)}) collective-permute-start(bf16[320,128]{1,0:T(8,128)(2,1)S(1)} %slice.76), channel_id=1, source_target_pairs={{0,2},{2,0},{4,6},{6,4},{8,10},{10,8},{12,14},{14,12},{1,3},{3,1},... | collective-permute-start | bytes 245768 | tf_op jit(solution)/shard_map/ppermute | solution.py:309
  12.2 6.0 %collective-permute-start.3 = (bf16[320,128]{1,0:T(8,128)(2,1)S(1)}, bf16[320,128]{1,0:T(8,128)(2,1)S(1)}, u32[]{:S(2)}, u32[]{:S(2)}) collective-permute-start(bf16[320,128]{1,0:T(8,128)(2,1)S(1)} %slice.77), channel_id=1, source_target_pairs={{0,2},{2,0},{4,6},{6,4},{8,10},{10,8},{12,14},{14,12},{1,3},{3,1},... | collective-permute-start | bytes 245768 | tf_op jit(solution)/shard_map/ppermute | solution.py:309
  14.5 4.4 %collective-permute-start.5 = (bf16[320,128]{1,0:T(8,128)(2,1)S(1)}, bf16[320,128]{1,0:T(8,128)(2,1)S(1)}, u32[]{:S(2)}, u32[]{:S(2)}) collective-permute-start(bf16[320,128]{1,0:T(8,128)(2,1)S(1)} %slice.78), channel_id=1, source_target_pairs={{0,2},{2,0},{4,6},{6,4},{8,10},{10,8},{12,14},{14,12},{1,3},{3,1},... | collective-permute-start | bytes 245768 | tf_op jit(solution)/shard_map/ppermute | solution.py:309
  24.0 5.2 %collective-permute-start.12 = (bf16[288,128]{1,0:T(8,128)(2,1)S(1)}, bf16[288,128]{1,0:T(8,128)(2,1)S(1)}, u32[]{:S(2)}, u32[]{:S(2)}) collective-permute-start(bf16[288,128]{1,0:T(8,128)(2,1)S(1)} %get-tuple-element.34), channel_id=1, source_target_pairs={{0,2},{2,0},{4,6},{6,4},{8,10},{10,8},{12,14},{14,12},{1,3},{3,1},... | collective-permute-start | bytes 221192 | tf_op jit(solution)/shard_map/ppermute | solution.py:309
  25.7 6.4 %collective-permute-start.10 = (bf16[288,128]{1,0:T(8,128)(2,1)S(1)}, bf16[288,128]{1,0:T(8,128)(2,1)S(1)}, u32[]{:S(2)}, u32[]{:S(2)}) collective-permute-start(bf16[288,128]{1,0:T(8,128)(2,1)S(1)} %get-tuple-element.32), channel_id=1, source_target_pairs={{0,2},{2,0},{4,6},{6,4},{8,10},{10,8},{12,14},{14,12},{1,3},{3,1},... | collective-permute-start | bytes 221192 | tf_op jit(solution)/shard_map/ppermute | solution.py:309
  26.1 6.1 %collective-permute-start.8 = (bf16[288,128]{1,0:T(8,128)(2,1)S(1)}, bf16[288,128]{1,0:T(8,128)(2,1)S(1)}, u32[]{:S(2)}, u32[]{:S(2)}) collective-permute-start(bf16[288,128]{1,0:T(8,128)(2,1)S(1)} %get-tuple-element.30), channel_id=1, source_target_pairs={{0,2},{2,0},{4,6},{6,4},{8,10},{10,8},{12,14},{14,12},{1,3},{3,1},... | collective-permute-start | bytes 221192 | tf_op jit(solution)/shard_map/ppermute | solution.py:309
  27.7 6.5 %collective-permute-start.7 = (bf16[288,128]{1,0:T(8,128)(2,1)S(1)}, bf16[288,128]{1,0:T(8,128)(2,1)S(1)}, u32[]{:S(2)}, u32[]{:S(2)}) collective-permute-start(bf16[288,128]{1,0:T(8,128)(2,1)S(1)} %get-tuple-element.28), channel_id=1, source_target_pairs={{0,2},{2,0},{4,6},{6,4},{8,10},{10,8},{12,14},{14,12},{1,3},{3,1},... | collective-permute-start | bytes 221192 | tf_op jit(solution)/shard_map/ppermute | solution.py:309
  29.4 6.4 %collective-permute-start.13 = (bf16[320,128]{1,0:T(8,128)(2,1)S(1)}, bf16[320,128]{1,0:T(8,128)(2,1)S(1)}, u32[]{:S(2)}, u32[]{:S(2)}) collective-permute-start(bf16[320,128]{1,0:T(8,128)(2,1)S(1)} %pad_maximum_fusion.3), channel_id=1, source_target_pairs={{0,12},{2,14},{4,8},{6,10},{8,4},{10,6},{12,0},{14,2},{1,13},{3,15... | collective-permute-start | bytes 245768 | tf_op jit(solution)/shard_map/ppermute | solution.py:309
  32.2 5.5 %collective-permute-start.11 = (bf16[320,128]{1,0:T(8,128)(2,1)S(1)}, bf16[320,128]{1,0:T(8,128)(2,1)S(1)}, u32[]{:S(2)}, u32[]{:S(2)}) collective-permute-start(bf16[320,128]{1,0:T(8,128)(2,1)S(1)} %pad_maximum_fusion.2), channel_id=1, source_target_pairs={{0,8},{2,10},{4,12},{6,14},{8,0},{10,2},{12,4},{14,6},{1,9},{3,11}... | collective-permute-start | bytes 245768 | tf_op jit(solution)/shard_map/ppermute | solution.py:309
  32.4 5.4 %collective-permute-start.9 = (bf16[320,128]{1,0:T(8,128)(2,1)S(1)}, bf16[320,128]{1,0:T(8,128)(2,1)S(1)}, u32[]{:S(2)}, u32[]{:S(2)}) collective-permute-start(bf16[320,128]{1,0:T(8,128)(2,1)S(1)} %pad_maximum_fusion.1), channel_id=1, source_target_pairs={{0,4},{2,6},{4,0},{6,2},{8,12},{10,14},{12,8},{14,10},{1,5},{3,7},... | collective-permute-start | bytes 245768 | tf_op jit(solution)/shard_map/ppermute | solution.py:309

commit v4 on v3

--- a/solution.py
+++ b/solution.py
@@ -118,13 +118,19 @@
     )(after, tiles)
 
 
-def adjoint_kernel(order, rows, epochs, group, table_ref, *refs):
+def adjoint_kernel(order, packs, rows, epochs, group, table_ref, *refs):
     peers = len(order)
     piece_refs = [refs[order.index(p)] for p in range(peers)]
     early_ref, tiles_ref = refs[peers : peers + 2]
-    out_refs = refs[peers + 2 : 2 * peers + 2]
-    late_ref, emission, loss, collected, sems = refs[2 * peers + 2 :]
+    out_refs = refs[peers + 2 : peers + 2 + len(packs)]
+    late_ref, emission, loss, collected, sems = refs[peers + 2 + len(packs) :]
     blocks_all, samples, side = emission.shape[0] - 1, emission.shape[1], emission.shape[2]
+    out_rows = (blocks_all + rows) * epochs
+    outs = [
+        (p, ref, place * out_rows)
+        for pack, ref in zip(packs, out_refs)
+        for place, p in enumerate(pack)
+    ]
     early, slots = early_ref.shape[:2]
     loads = [
         pltpu.make_async_copy(tiles_ref.at[early + r], late_ref.at[r], sems.at[r])
@@ -204,19 +210,20 @@
     def _(quad):
         step = pl.multiple_of(quad * 4 * epochs, 4 * epochs)
         parts = [collected[quad * 4 + c] for c in range(4)]
-        for p, ref in enumerate(out_refs):
-            ref[pl.ds(step, 4 * epochs), :] = jnp.concatenate(
+        for p, ref, base in outs:
+            ref[pl.ds(base + step, 4 * epochs), :] = jnp.concatenate(
                 [part[p * epochs : (p + 1) * epochs] for part in parts], 0
             ).astype(BF16)
 
     for first in range(0, rows, 4):
         parts = [collected[me * rows + first + c] for c in range(4)]
-        for p, ref in enumerate(out_refs):
+        for p, ref, base in outs:
             full = jnp.concatenate([part[p * epochs : (p + 1) * epochs] for part in parts], 0)
-            ref[wide + first * epochs : wide + (first + 4) * epochs, :] = halves(full)[1]
-
-
-def adjoint_terms(table, order, pieces, early, tiles, epochs, blocks_all):
+            base += wide + first * epochs
+            ref[base : base + 4 * epochs, :] = halves(full)[1]
+
+
+def adjoint_terms(table, order, packs, pieces, early, tiles, epochs, blocks_all):
     peers = len(pieces)
     rows, slots, side = tiles.shape[:3]
     samples = peers * epochs
@@ -228,11 +235,11 @@
         + rows * samples * side * 4
     )
     return pl.pallas_call(
-        functools.partial(adjoint_kernel, order, rows, epochs, min(8, slots)),
+        functools.partial(adjoint_kernel, order, packs, rows, epochs, min(8, slots)),
         in_specs=[pl.BlockSpec(memory_space=pltpu.SMEM)]
         + [RESIDENT] * (peers + 1)
         + [pl.BlockSpec(memory_space=pl.ANY)],
-        out_specs=[RESIDENT] * peers,
+        out_specs=[RESIDENT] * len(packs),
         scratch_shapes=[
             pltpu.VMEM((rows - early.shape[0], *tiles.shape[1:]), BF16),
             pltpu.VMEM((blocks_all + 1, samples, side), BF16),
@@ -240,7 +247,7 @@
             pltpu.VMEM((blocks_all + 1, samples, side), F32),
             pltpu.SemaphoreType.DMA((rows - early.shape[0],)),
         ],
-        out_shape=[jax.ShapeDtypeStruct((out_rows, side), BF16)] * peers,
+        out_shape=[jax.ShapeDtypeStruct((out_rows * len(pack), side), BF16) for pack in packs],
         compiler_params=pltpu.CompilerParams(vmem_limit_bytes=need + (6 << 20)),
         cost_estimate=pl.CostEstimate(
             flops=4 * rows * slots * side * side * samples,
@@ -250,24 +257,26 @@
     )(table, *[pieces[p] for p in order], early, tiles)
 
 
-def finish_kernel(steps, rows, epochs, scale_ref, *refs):
-    sum_refs, out_ref, total = refs[: len(steps)], refs[-2], refs[-1]
+def finish_kernel(owners, rows, epochs, scale_ref, *refs):
+    sum_refs, out_ref, total = refs[: len(owners)], refs[-2], refs[-1]
     wide, side = total.shape
-    part = 2 * rows * epochs
-    pair = lax.axis_index("node") // 2
+    part = rows * epochs
+    me = lax.axis_index("node")
     total[...] = sum(ref[:wide, :].astype(F32) for ref in sum_refs)
-    for p, ref in zip(steps, sum_refs):
-        span = pl.ds(pl.multiple_of((pair ^ (p // 2)) * part, part), part)
-        total[span, :] += ref[wide:, :].astype(F32)
+    for steps, ref in zip(owners, sum_refs):
+        for place, step in enumerate(steps):
+            span = pl.ds(pl.multiple_of((me ^ step) * part, part), part)
+            start = wide + place * part
+            total[span, :] += ref[start : start + part, :].astype(F32)
     for c in range(wide // epochs):
         span = slice(c * epochs, (c + 1) * epochs)
         out_ref[:, c * side : (c + 1) * side] = scale_ref[span, :] * total[span, :]
 
 
-def finish(steps, rows, epochs, scale, sums):
+def finish(owners, rows, epochs, scale, sums):
     wide, side = scale.shape
     return pl.pallas_call(
-        functools.partial(finish_kernel, steps, rows, epochs),
+        functools.partial(finish_kernel, owners, rows, epochs),
         in_specs=[RESIDENT] * (1 + len(sums)),
         out_specs=RESIDENT,
         scratch_shapes=[pltpu.VMEM((wide, side), F32)],
@@ -276,18 +285,16 @@
     )(scale, *sums)
 
 
-def add_neighbour(me, wide, mine, theirs):
+def add_terms_of(node, other, wide, mine, theirs):
+    part = mine.shape[0] - wide
     total = mine[:wide].astype(F32) + theirs[:wide].astype(F32)
-    low_mine, low_theirs = mine[wide:].astype(F32), theirs[wide:].astype(F32)
-    odd = me % 2 == 1
-    low = jnp.concatenate(
-        [jnp.where(odd, low_theirs, low_mine), jnp.where(odd, low_mine, low_theirs)], 0
-    )
-    start = (me // 2) * low.shape[0]
-    window = lax.dynamic_slice_in_dim(total, start, low.shape[0], 0) + low
-    high = lax.reduce_precision(window, 8, 7)
-    total = lax.dynamic_update_slice_in_dim(total.astype(BF16), high.astype(BF16), start, 0)
-    return jnp.concatenate([total, (window - high).astype(BF16)], 0)
+    rounded, rest = total.astype(BF16), []
+    for owner, low in ((node, mine[wide:]), (other, theirs[wide:])):
+        window = lax.dynamic_slice_in_dim(total, owner * part, part, 0) + low.astype(F32)
+        high = lax.reduce_precision(window, 8, 7)
+        rounded = lax.dynamic_update_slice_in_dim(rounded, high.astype(BF16), owner * part, 0)
+        rest.append((window - high).astype(BF16))
+    return jnp.concatenate([rounded, *rest], 0)
 
 
 def on_device(
@@ -329,13 +336,24 @@
     order = tuple(q for d in near for q in (2 * d + 1, 2 * d))
     tiles = pltpu.with_memory_space_constraint(gebhart_tiles, pltpu.HBM)
     early = load_tiles(tiles, pieces[far[0]], rows // 2)
-    terms = adjoint_terms(table, order, pieces, early, tiles, epochs, blocks_all)
-
-    steps = tuple(range(0, nodes, 2))
-    arrived = {p: send(terms[p ^ 1], 1) for p in steps}
-    paired = {p: add_neighbour(me, wide, terms[p], arrived[p]) for p in steps}
-    sums = [paired[0]] + [send(paired[p], p) for p in steps[1:]]
-    return finish(steps, rows, epochs, scale, sums)
+    distant = range(4, nodes, 2)
+    packs = (*((p,) for p in (*distant, *(p + 1 for p in distant), 0, 1)), (2, 3))
+    terms = adjoint_terms(table, order, packs, pieces, early, tiles, epochs, blocks_all)
+    terms = dict(zip(packs, terms))
+
+    def add(step, mine, theirs):
+        return add_terms_of(me, me ^ step, wide, mine, theirs)
+
+    arrived = {p: send(terms[(p + 1,)], 1) for p in distant}
+    near = jnp.split(send(terms[(2, 3)], 2), 2)
+    sums = {p: send(add(1, terms[(p,)], arrived[p]), p) for p in distant}
+    sums[1] = send(add(2, terms[(1,)], near[1]), 1)
+    sums[0] = add(2, terms[(0,)], near[0])
+    steps = (*distant, 1, 0)
+    owners = {p: (p, p ^ 2 if p < 2 else p ^ 1) for p in steps}
+    return finish(
+        [owners[p] for p in steps], rows, epochs, scale, [sums[p] for p in steps]
+    )
 
 
 def solution(mesh):

time: 38.7 us -> 38.3 us (0.990)
  starting transfers between devices: 20.9 us -> 20.3 us
    ppermute x14 -> x13, starting transfers between devices: 20.9 us -> 20.3 us  [send(): return lax.ppermute(value, 'node', [(i, i ^ step) for i in range(nodes)])]
    ppermute x14 -> x13, waiting for transfers between devices: 7.99 us -> 8.26 us  [send(): return lax.ppermute(value, 'node', [(i, i ^ step) for i in range(nodes)])]
  transfers between devices with their start and end apart: 14 -> 13, of which waited for: 8 -> 8; matrix products, arithmetic and copies ran while one was open for 1% -> 1% of each run, Pallas kernels for 6% -> 6%
where the time goes in v4:
time: 38.3 us; the launch traced here: 38.2 us
  starting transfers between devices  20.3 us (53%)
  Pallas kernels  9.18 us (24%)
  waiting for transfers between devices  8.26 us (22%)
    ppermute x13, starting transfers between devices, send(): return lax.ppermute(value, 'node', [(i, i ^ step) for i in range(nodes)])  20.3 us
    ppermute x13, waiting for transfers between devices, send(): return lax.ppermute(value, 'node', [(i, i ^ step) for i in range(nodes)])  8.26 us
    pallas_call x1, Pallas kernels, adjoint_terms(): pl.pallas_call(functools.partial(adjoint_kernel, order, packs, rows, epoc...  5.14 us
    pallas_call x1, Pallas kernels, load_tiles(): pl.pallas_call(load_kernel, in_specs=[pl.BlockSpec(memory_space=pl.ANY)]...  2.2 us
    pallas_call x1, Pallas kernels, prepare(): pl.pallas_call(functools.partial(prepare_kernel, far, rows), grid=(1,), i...  1.09 us
  transfers between devices with their start and end apart: 13, of which 8 were waited for; matrix products, arithmetic and copies ran while one was open for 1% of the time, Pallas kernels for 6%

profile of v4, /device:TPU:0, one launch (start us, length us, event | category | flops | bytes accessed | tf_op | source)
XLA Modules:
  0.0 38.2 jit_solution(2950903980302427526)
XLA Ops:
  0.0 1.1 %shard_map.64 = (bf16[384,128]{1,0:T(8,128)(2,1)S(1)}, bf16[384,128]{1,0:T(8,128)(2,1)S(1)}, bf16[384,128]{1,0:T(8,128)(2,1)S(1)}, bf16[320,128]{1,0:T(8,128)(2,...) custom-call(f32[4,8192]{1,0:T(4,128)} %kelvin_ref.1, f32[64,128]{1,0:T(8,128)} %bitcast.1, ...), custom_call_target="tpu_custom_call" | custom-call | tf_op jit(solution)/shard_map/pallas_call | solution.py:84
  1.1 5.1 %collective-permute-start = (bf16[384,128]{1,0:T(8,128)(2,1)S(1)}, bf16[384,128]{1,0:T(8,128)(2,1)S(1)}, u32[]{:S(2)}, u32[]{:S(2)}) collective-permute-start(bf16[384,128]{1,0:T(8,128)(2,1)S(1)} %get-tuple-element.21), channel_id=1, source_target_pairs={{0,12},{2,14},{4,8},{6,10},{8,4},{10,6},{12,0},{14,2},{1,13},{3,15... | collective-permute-start | bytes 294920 | tf_op jit(solution)/shard_map/ppermute | solution.py:316
  6.2 0.6 %collective-permute-start.4 = (bf16[384,128]{1,0:T(8,128)(2,1)S(1)}, bf16[384,128]{1,0:T(8,128)(2,1)S(1)}, u32[]{:S(2)}, u32[]{:S(2)}) collective-permute-start(bf16[384,128]{1,0:T(8,128)(2,1)S(1)} %get-tuple-element.23), channel_id=1, source_target_pairs={{0,8},{2,10},{4,12},{6,14},{8,0},{10,2},{12,4},{14,6},{1,9},{3,11}... | collective-permute-start | bytes 294920 | tf_op jit(solution)/shard_map/ppermute | solution.py:316
  6.9 1.7 %collective-permute-start.6 = (bf16[320,128]{1,0:T(8,128)(2,1)S(1)}, bf16[320,128]{1,0:T(8,128)(2,1)S(1)}, u32[]{:S(2)}, u32[]{:S(2)}) collective-permute-start(bf16[320,128]{1,0:T(8,128)(2,1)S(1)} %get-tuple-element.24), channel_id=1, source_target_pairs={{0,2},{2,0},{4,6},{6,4},{8,10},{10,8},{12,14},{14,12},{1,3},{3,1},... | collective-permute-start | bytes 245768 | tf_op jit(solution)/shard_map/ppermute | solution.py:316
  8.5 1.4 %collective-permute-done.after_ref.refs_1_ = bf16[384,128]{1,0:T(8,128)(2,1)S(1)} collective-permute-done((bf16[384,128]{1,0:T(8,128)(2,1)S(1)}, bf16[384,128]{1,0:T(8,128)(2,1)S(1)}, u32[]{:S(2)}, u32[]{:S(2)}) %collective-permute-start) | collective-permute-done | bytes 98336 | tf_op jit(solution)/shard_map/ppermute | solution.py:316
  9.9 1.7 %collective-permute-start.1 = (bf16[320,128]{1,0:T(8,128)(2,1)S(1)}, bf16[320,128]{1,0:T(8,128)(2,1)S(1)}, u32[]{:S(2)}, u32[]{:S(2)}) collective-permute-start(bf16[320,128]{1,0:T(8,128)(2,1)S(1)} %slice.80), channel_id=1, source_target_pairs={{0,2},{2,0},{4,6},{6,4},{8,10},{10,8},{12,14},{14,12},{1,3},{3,1},... | collective-permute-start | bytes 245768 | tf_op jit(solution)/shard_map/ppermute | solution.py:316
  11.6 0.6 %collective-permute-done.2.refs_3_ = bf16[384,128]{1,0:T(8,128)(2,1)S(1)} collective-permute-done((bf16[384,128]{1,0:T(8,128)(2,1)S(1)}, bf16[384,128]{1,0:T(8,128)(2,1)S(1)}, u32[]{:S(2)}, u32[]{:S(2)}) %collective-permute-start.2) | collective-permute-done | bytes 98336 | tf_op jit(solution)/shard_map/ppermute | solution.py:316
  12.2 1.5 %collective-permute-start.3 = (bf16[320,128]{1,0:T(8,128)(2,1)S(1)}, bf16[320,128]{1,0:T(8,128)(2,1)S(1)}, u32[]{:S(2)}, u32[]{:S(2)}) collective-permute-start(bf16[320,128]{1,0:T(8,128)(2,1)S(1)} %slice.81), channel_id=1, source_target_pairs={{0,2},{2,0},{4,6},{6,4},{8,10},{10,8},{12,14},{14,12},{1,3},{3,1},... | collective-permute-start | bytes 245768 | tf_op jit(solution)/shard_map/ppermute | solution.py:316
  13.8 0.7 %collective-permute-done.4.refs_5_ = bf16[384,128]{1,0:T(8,128)(2,1)S(1)} collective-permute-done((bf16[384,128]{1,0:T(8,128)(2,1)S(1)}, bf16[384,128]{1,0:T(8,128)(2,1)S(1)}, u32[]{:S(2)}, u32[]{:S(2)}) %collective-permute-start.4) | collective-permute-done | bytes 98336 | tf_op jit(solution)/shard_map/ppermute | solution.py:316
  14.5 1.5 %collective-permute-start.5 = (bf16[320,128]{1,0:T(8,128)(2,1)S(1)}, bf16[320,128]{1,0:T(8,128)(2,1)S(1)}, u32[]{:S(2)}, u32[]{:S(2)}) collective-permute-start(bf16[320,128]{1,0:T(8,128)(2,1)S(1)} %slice.82), channel_id=1, source_target_pairs={{0,2},{2,0},{4,6},{6,4},{8,10},{10,8},{12,14},{14,12},{1,3},{3,1},... | collective-permute-start | bytes 245768 | tf_op jit(solution)/shard_map/ppermute | solution.py:316
  16.0 2.2 %shard_map.65.refs_8_ = bf16[4,32,128,128]{3,2,1,0:T(8,128)(2,1)S(1)} custom-call(bf16[384,128]{1,0:T(8,128)(2,1)S(1)} %collective-permute-done.after_ref.refs_1_, bf16[8,32,128,128]{3,2,1,0:T(8,128)(2,1)} %refs_9_.1), custom_call_target="tpu_custom_call" | custom-call | bytes 16777216 | tf_op jit(solution)/shard_map/pallas_call | solution.py:108
  18.3 0.7 %collective-permute-done.5.refs_4_ = bf16[320,128]{1,0:T(8,128)(2,1)S(1)} collective-permute-done((bf16[320,128]{1,0:T(8,128)(2,1)S(1)}, bf16[320,128]{1,0:T(8,128)(2,1)S(1)}, u32[]{:S(2)}, u32[]{:S(2)}) %collective-permute-start.5) | collective-permute-done | bytes 81952 | tf_op jit(solution)/shard_map/ppermute | solution.py:316
  18.9 5.1 %shard_map.66 = (bf16[288,128]{1,0:T(8,128)(2,1)S(1)}, bf16[288,128]{1,0:T(8,128)(2,1)S(1)}, bf16[288,128]{1,0:T(8,128)(2,1)S(1)}, bf16[288,128]{1,0:T(8,128)(2,...) custom-call(s32[8,32]{1,0:T(8,128)S(1)} %get-tuple-element.20.table_ref, ...), custom_call_target="tpu_custom_call" | custom-call | flops 536870912 | bytes 8388608 | tf_op jit(solution)/shard_map/pallas_call | solution.py:237
  24.1 1.6 %collective-permute-start.7 = (bf16[288,128]{1,0:T(8,128)(2,1)S(1)}, bf16[288,128]{1,0:T(8,128)(2,1)S(1)}, u32[]{:S(2)}, u32[]{:S(2)}) collective-permute-start(bf16[288,128]{1,0:T(8,128)(2,1)S(1)} %get-tuple-element.27), channel_id=1, source_target_pairs={{0,2},{2,0},{4,6},{6,4},{8,10},{10,8},{12,14},{14,12},{1,3},{3,1},... | collective-permute-start | bytes 221192 | tf_op jit(solution)/shard_map/ppermute | solution.py:316
  25.7 0.5 %collective-permute-start.9 = (bf16[288,128]{1,0:T(8,128)(2,1)S(1)}, bf16[288,128]{1,0:T(8,128)(2,1)S(1)}, u32[]{:S(2)}, u32[]{:S(2)}) collective-permute-start(bf16[288,128]{1,0:T(8,128)(2,1)S(1)} %get-tuple-element.29), channel_id=1, source_target_pairs={{0,2},{2,0},{4,6},{6,4},{8,10},{10,8},{12,14},{14,12},{1,3},{3,1},... | collective-permute-start | bytes 221192 | tf_op jit(solution)/shard_map/ppermute | solution.py:316
  26.2 1.1 %collective-permute-start.11 = (bf16[576,128]{1,0:T(8,128)(2,1)S(1)}, bf16[576,128]{1,0:T(8,128)(2,1)S(1)}, u32[]{:S(2)}, u32[]{:S(2)}) collective-permute-start(bf16[576,128]{1,0:T(8,128)(2,1)S(1)} %get-tuple-element.31), channel_id=1, source_target_pairs={{0,4},{2,6},{4,0},{6,2},{8,12},{10,14},{12,8},{14,10},{1,5},{3,7},... | collective-permute-start | bytes 442376 | tf_op jit(solution)/shard_map/ppermute | solution.py:316
  27.3 1.2 %collective-permute-done.7 = bf16[288,128]{1,0:T(8,128)(2,1)S(1)} collective-permute-done((bf16[288,128]{1,0:T(8,128)(2,1)S(1)}, bf16[288,128]{1,0:T(8,128)(2,1)S(1)}, u32[]{:S(2)}, u32[]{:S(2)}) %collective-permute-start.7) | collective-permute-done | bytes 73760 | tf_op jit(solution)/shard_map/ppermute | solution.py:316
  28.6 1.5 %collective-permute-start.8 = (bf16[320,128]{1,0:T(8,128)(2,1)S(1)}, bf16[320,128]{1,0:T(8,128)(2,1)S(1)}, u32[]{:S(2)}, u32[]{:S(2)}) collective-permute-start(bf16[320,128]{1,0:T(8,128)(2,1)S(1)} %pad_maximum_fusion), channel_id=1, source_target_pairs={{0,8},{2,10},{4,12},{6,14},{8,0},{10,2},{12,4},{14,6},{1,9},{3,11}... | collective-permute-start | bytes 245768 | tf_op jit(solution)/shard_map/ppermute | solution.py:316
  30.3 2.5 %collective-permute-start.10 = (bf16[320,128]{1,0:T(8,128)(2,1)S(1)}, bf16[320,128]{1,0:T(8,128)(2,1)S(1)}, u32[]{:S(2)}, u32[]{:S(2)}) collective-permute-start(bf16[320,128]{1,0:T(8,128)(2,1)S(1)} %pad_maximum_fusion.1), channel_id=1, source_target_pairs={{0,12},{2,14},{4,8},{6,10},{8,4},{10,6},{12,0},{14,2},{1,13},{3,15... | collective-permute-start | bytes 245768 | tf_op jit(solution)/shard_map/ppermute | solution.py:316
  32.9 0.9 %collective-permute-start.12 = (bf16[320,128]{1,0:T(8,128)(2,1)S(1)}, bf16[320,128]{1,0:T(8,128)(2,1)S(1)}, u32[]{:S(2)}, u32[]{:S(2)}) collective-permute-start(bf16[320,128]{1,0:T(8,128)(2,1)S(1)} %pad_maximum_fusion.2), channel_id=1, source_target_pairs={{0,2},{2,0},{4,6},{6,4},{8,10},{10,8},{12,14},{14,12},{1,3},{3,1},... | collective-permute-start | bytes 245768 | tf_op jit(solution)/shard_map/ppermute | solution.py:316
  33.8 1.6 %collective-permute-done.8.refs_0_ = bf16[320,128]{1,0:T(8,128)(2,1)S(1)} collective-permute-done((bf16[320,128]{1,0:T(8,128)(2,1)S(1)}, bf16[320,128]{1,0:T(8,128)(2,1)S(1)}, u32[]{:S(2)}, u32[]{:S(2)}) %collective-permute-start.8) | collective-permute-done | bytes 81952 | tf_op jit(solution)/shard_map/ppermute | solution.py:316
  35.4 1.2 %collective-permute-done.10.refs_1_ = bf16[320,128]{1,0:T(8,128)(2,1)S(1)} collective-permute-done((bf16[320,128]{1,0:T(8,128)(2,1)S(1)}, bf16[320,128]{1,0:T(8,128)(2,1)S(1)}, u32[]{:S(2)}, u32[]{:S(2)}) %collective-permute-start.10) | collective-permute-done | bytes 81952 | tf_op jit(solution)/shard_map/ppermute | solution.py:316
  36.7 0.8 %collective-permute-done.12.refs_2_ = bf16[320,128]{1,0:T(8,128)(2,1)S(1)} collective-permute-done((bf16[320,128]{1,0:T(8,128)(2,1)S(1)}, bf16[320,128]{1,0:T(8,128)(2,1)S(1)}, u32[]{:S(2)}, u32[]{:S(2)}) %collective-permute-start.12) | collective-permute-done | bytes 81952 | tf_op jit(solution)/shard_map/ppermute | solution.py:316
  37.4 0.7 %shard_map.67 = f32[4,8192]{1,0:T(4,128)} custom-call(f32[256,128]{1,0:T(8,128)S(1)} %get-tuple-element.19.scale_ref, bf16[320,128]{1,0:T(8,128)(2,1)S(1)} %collective-permute-done.8.refs_0_, bf16[320,128]{1,0:T(8,128)(2,1)S(1)} %collective-permute-done.10.refs_1_, bf16[320,128]{1,0:T(8,128)(2,1)S(1)} %collective-permute-done.12.refs_2_, ...), custom_call_target="tpu_custom_call" | custom-call | tf_op jit(solution)/shard_map/pallas_call | solution.py:278
  (25 shorter events, 0.3 us)
Async XLA Ops:
  1.1 8.8 %collective-permute-start = (bf16[384,128]{1,0:T(8,128)(2,1)S(1)}, bf16[384,128]{1,0:T(8,128)(2,1)S(1)}, u32[]{:S(2)}, u32[]{:S(2)}) collective-permute-start(bf16[384,128]{1,0:T(8,128)(2,1)S(1)} %get-tuple-element.21), channel_id=1, source_target_pairs={{0,12},{2,14},{4,8},{6,10},{8,4},{10,6},{12,0},{14,2},{1,13},{3,15... | collective-permute-start | bytes 294920 | tf_op jit(solution)/shard_map/ppermute | solution.py:316
  6.2 6.0 %collective-permute-start.2 = (bf16[384,128]{1,0:T(8,128)(2,1)S(1)}, bf16[384,128]{1,0:T(8,128)(2,1)S(1)}, u32[]{:S(2)}, u32[]{:S(2)}) collective-permute-start(bf16[384,128]{1,0:T(8,128)(2,1)S(1)} %get-tuple-element.22), channel_id=1, source_target_pairs={{0,4},{2,6},{4,0},{6,2},{8,12},{10,14},{12,8},{14,10},{1,5},{3,7},... | collective-permute-start | bytes 294920 | tf_op jit(solution)/shard_map/ppermute | solution.py:316
  6.2 8.3 %collective-permute-start.4 = (bf16[384,128]{1,0:T(8,128)(2,1)S(1)}, bf16[384,128]{1,0:T(8,128)(2,1)S(1)}, u32[]{:S(2)}, u32[]{:S(2)}) collective-permute-start(bf16[384,128]{1,0:T(8,128)(2,1)S(1)} %get-tuple-element.23), channel_id=1, source_target_pairs={{0,8},{2,10},{4,12},{6,14},{8,0},{10,2},{12,4},{14,6},{1,9},{3,11}... | collective-permute-start | bytes 294920 | tf_op jit(solution)/shard_map/ppermute | solution.py:316
  6.9 11.4 %collective-permute-start.6 = (bf16[320,128]{1,0:T(8,128)(2,1)S(1)}, bf16[320,128]{1,0:T(8,128)(2,1)S(1)}, u32[]{:S(2)}, u32[]{:S(2)}) collective-permute-start(bf16[320,128]{1,0:T(8,128)(2,1)S(1)} %get-tuple-element.24), channel_id=1, source_target_pairs={{0,2},{2,0},{4,6},{6,4},{8,10},{10,8},{12,14},{14,12},{1,3},{3,1},... | collective-permute-start | bytes 245768 | tf_op jit(solution)/shard_map/ppermute | solution.py:316
  9.9 8.3 %collective-permute-start.1 = (bf16[320,128]{1,0:T(8,128)(2,1)S(1)}, bf16[320,128]{1,0:T(8,128)(2,1)S(1)}, u32[]{:S(2)}, u32[]{:S(2)}) collective-permute-start(bf16[320,128]{1,0:T(8,128)(2,1)S(1)} %slice.80), channel_id=1, source_target_pairs={{0,2},{2,0},{4,6},{6,4},{8,10},{10,8},{12,14},{14,12},{1,3},{3,1},... | collective-permute-start | bytes 245768 | tf_op jit(solution)/shard_map/ppermute | solution.py:316
  12.2 6.0 %collective-permute-start.3 = (bf16[320,128]{1,0:T(8,128)(2,1)S(1)}, bf16[320,128]{1,0:T(8,128)(2,1)S(1)}, u32[]{:S(2)}, u32[]{:S(2)}) collective-permute-start(bf16[320,128]{1,0:T(8,128)(2,1)S(1)} %slice.81), channel_id=1, source_target_pairs={{0,2},{2,0},{4,6},{6,4},{8,10},{10,8},{12,14},{14,12},{1,3},{3,1},... | collective-permute-start | bytes 245768 | tf_op jit(solution)/shard_map/ppermute | solution.py:316
  14.5 4.4 %collective-permute-start.5 = (bf16[320,128]{1,0:T(8,128)(2,1)S(1)}, bf16[320,128]{1,0:T(8,128)(2,1)S(1)}, u32[]{:S(2)}, u32[]{:S(2)}) collective-permute-start(bf16[320,128]{1,0:T(8,128)(2,1)S(1)} %slice.82), channel_id=1, source_target_pairs={{0,2},{2,0},{4,6},{6,4},{8,10},{10,8},{12,14},{14,12},{1,3},{3,1},... | collective-permute-start | bytes 245768 | tf_op jit(solution)/shard_map/ppermute | solution.py:316
  24.1 4.4 %collective-permute-start.7 = (bf16[288,128]{1,0:T(8,128)(2,1)S(1)}, bf16[288,128]{1,0:T(8,128)(2,1)S(1)}, u32[]{:S(2)}, u32[]{:S(2)}) collective-permute-start(bf16[288,128]{1,0:T(8,128)(2,1)S(1)} %get-tuple-element.27), channel_id=1, source_target_pairs={{0,2},{2,0},{4,6},{6,4},{8,10},{10,8},{12,14},{14,12},{1,3},{3,1},... | collective-permute-start | bytes 221192 | tf_op jit(solution)/shard_map/ppermute | solution.py:316
  25.7 4.5 %collective-permute-start.9 = (bf16[288,128]{1,0:T(8,128)(2,1)S(1)}, bf16[288,128]{1,0:T(8,128)(2,1)S(1)}, u32[]{:S(2)}, u32[]{:S(2)}) collective-permute-start(bf16[288,128]{1,0:T(8,128)(2,1)S(1)} %get-tuple-element.29), channel_id=1, source_target_pairs={{0,2},{2,0},{4,6},{6,4},{8,10},{10,8},{12,14},{14,12},{1,3},{3,1},... | collective-permute-start | bytes 221192 | tf_op jit(solution)/shard_map/ppermute | solution.py:316
  26.2 6.6 %collective-permute-start.11 = (bf16[576,128]{1,0:T(8,128)(2,1)S(1)}, bf16[576,128]{1,0:T(8,128)(2,1)S(1)}, u32[]{:S(2)}, u32[]{:S(2)}) collective-permute-start(bf16[576,128]{1,0:T(8,128)(2,1)S(1)} %get-tuple-element.31), channel_id=1, source_target_pairs={{0,4},{2,6},{4,0},{6,2},{8,12},{10,14},{12,8},{14,10},{1,5},{3,7},... | collective-permute-start | bytes 442376 | tf_op jit(solution)/shard_map/ppermute | solution.py:316
  28.6 6.8 %collective-permute-start.8 = (bf16[320,128]{1,0:T(8,128)(2,1)S(1)}, bf16[320,128]{1,0:T(8,128)(2,1)S(1)}, u32[]{:S(2)}, u32[]{:S(2)}) collective-permute-start(bf16[320,128]{1,0:T(8,128)(2,1)S(1)} %pad_maximum_fusion), channel_id=1, source_target_pairs={{0,8},{2,10},{4,12},{6,14},{8,0},{10,2},{12,4},{14,6},{1,9},{3,11}... | collective-permute-start | bytes 245768 | tf_op jit(solution)/shard_map/ppermute | solution.py:316
  30.3 6.4 %collective-permute-start.10 = (bf16[320,128]{1,0:T(8,128)(2,1)S(1)}, bf16[320,128]{1,0:T(8,128)(2,1)S(1)}, u32[]{:S(2)}, u32[]{:S(2)}) collective-permute-start(bf16[320,128]{1,0:T(8,128)(2,1)S(1)} %pad_maximum_fusion.1), channel_id=1, source_target_pairs={{0,12},{2,14},{4,8},{6,10},{8,4},{10,6},{12,0},{14,2},{1,13},{3,15... | collective-permute-start | bytes 245768 | tf_op jit(solution)/shard_map/ppermute | solution.py:316
  32.9 4.5 %collective-permute-start.12 = (bf16[320,128]{1,0:T(8,128)(2,1)S(1)}, bf16[320,128]{1,0:T(8,128)(2,1)S(1)}, u32[]{:S(2)}, u32[]{:S(2)}) collective-permute-start(bf16[320,128]{1,0:T(8,128)(2,1)S(1)} %pad_maximum_fusion.2), channel_id=1, source_target_pairs={{0,2},{2,0},{4,6},{6,4},{8,10},{10,8},{12,14},{14,12},{1,3},{3,1},... | collective-permute-start | bytes 245768 | tf_op jit(solution)/shard_map/ppermute | solution.py:316

commit v5 on v4

--- a/solution.py
+++ b/solution.py
@@ -258,7 +258,8 @@
 
 
 def finish_kernel(owners, rows, epochs, scale_ref, *refs):
-    sum_refs, out_ref, total = refs[: len(owners)], refs[-2], refs[-1]
+    sum_refs = refs[: len(owners)]
+    out_ref, total, result, sems = refs[len(owners) :]
     wide, side = total.shape
     part = rows * epochs
     me = lax.axis_index("node")
@@ -268,9 +269,18 @@
             span = pl.ds(pl.multiple_of((me ^ step) * part, part), part)
             start = wide + place * part
             total[span, :] += ref[start : start + part, :].astype(F32)
-    for c in range(wide // epochs):
-        span = slice(c * epochs, (c + 1) * epochs)
-        out_ref[:, c * side : (c + 1) * side] = scale_ref[span, :] * total[span, :]
+    blocks_all, copies = wide // epochs, []
+    for first in range(0, blocks_all, blocks_all // 4):
+        for c in range(first, first + blocks_all // 4):
+            span = slice(c * epochs, (c + 1) * epochs)
+            result[:, c * side : (c + 1) * side] = scale_ref[span, :] * total[span, :]
+        part = slice(first * side, (first + blocks_all // 4) * side)
+        copies.append(
+            pltpu.make_async_copy(result.at[:, part], out_ref.at[:, part], sems.at[len(copies)])
+        )
+        copies[-1].start()
+    for copy in copies:
+        copy.wait()
 
 
 def finish(owners, rows, epochs, scale, sums):
@@ -278,8 +288,12 @@
     return pl.pallas_call(
         functools.partial(finish_kernel, owners, rows, epochs),
         in_specs=[RESIDENT] * (1 + len(sums)),
-        out_specs=RESIDENT,
-        scratch_shapes=[pltpu.VMEM((wide, side), F32)],
+        out_specs=pl.BlockSpec(memory_space=pl.ANY),
+        scratch_shapes=[
+            pltpu.VMEM((wide, side), F32),
+            pltpu.VMEM((epochs, wide // epochs * side), F32),
+            pltpu.SemaphoreType.DMA((4,)),
+        ],
         out_shape=jax.ShapeDtypeStruct((epochs, wide // epochs * side), F32),
         compiler_params=pltpu.CompilerParams(vmem_limit_bytes=24 << 20),
     )(scale, *sums)

time: 38.3 us -> 38.3 us (level)
  no operation moved by 1% of the time
where the time goes in v5:
time: 38.3 us; the launch traced here: 38.1 us
  starting transfers between devices  20.6 us (54%)
  Pallas kernels  9.13 us (24%)
  waiting for transfers between devices  7.93 us (21%)
    ppermute x13, starting transfers between devices, send(): return lax.ppermute(value, 'node', [(i, i ^ step) for i in range(nodes)])  20.6 us
    ppermute x13, waiting for transfers between devices, send(): return lax.ppermute(value, 'node', [(i, i ^ step) for i in range(nodes)])  7.93 us
    pallas_call x1, Pallas kernels, adjoint_terms(): pl.pallas_call(functools.partial(adjoint_kernel, order, packs, rows, epoc...  5.08 us
    pallas_call x1, Pallas kernels, load_tiles(): pl.pallas_call(load_kernel, in_specs=[pl.BlockSpec(memory_space=pl.ANY)]...  2.2 us
    pallas_call x1, Pallas kernels, prepare(): pl.pallas_call(functools.partial(prepare_kernel, far, rows), grid=(1,), i...  1.09 us
  transfers between devices with their start and end apart: 13, of which 8 were waited for; matrix products, arithmetic and copies ran while one was open for 1% of the time, Pallas kernels for 6%

profile of v5, /device:TPU:0, one launch (start us, length us, event | category | flops | bytes accessed | tf_op | source)
XLA Modules:
  0.0 38.1 jit_solution(5204613388973803881)
XLA Ops:
  0.0 1.1 %shard_map.64 = (bf16[384,128]{1,0:T(8,128)(2,1)S(1)}, bf16[384,128]{1,0:T(8,128)(2,1)S(1)}, bf16[384,128]{1,0:T(8,128)(2,1)S(1)}, bf16[320,128]{1,0:T(8,128)(2,...) custom-call(f32[4,8192]{1,0:T(4,128)} %kelvin_ref.1, f32[64,128]{1,0:T(8,128)} %bitcast.1, ...), custom_call_target="tpu_custom_call" | custom-call | tf_op jit(solution)/shard_map/pallas_call | solution.py:84
  1.1 5.1 %collective-permute-start = (bf16[384,128]{1,0:T(8,128)(2,1)S(1)}, bf16[384,128]{1,0:T(8,128)(2,1)S(1)}, u32[]{:S(2)}, u32[]{:S(2)}) collective-permute-start(bf16[384,128]{1,0:T(8,128)(2,1)S(1)} %get-tuple-element.21), channel_id=1, source_target_pairs={{0,12},{2,14},{4,8},{6,10},{8,4},{10,6},{12,0},{14,2},{1,13},{3,15... | collective-permute-start | bytes 294920 | tf_op jit(solution)/shard_map/ppermute | solution.py:330
  6.2 0.6 %collective-permute-start.4 = (bf16[384,128]{1,0:T(8,128)(2,1)S(1)}, bf16[384,128]{1,0:T(8,128)(2,1)S(1)}, u32[]{:S(2)}, u32[]{:S(2)}) collective-permute-start(bf16[384,128]{1,0:T(8,128)(2,1)S(1)} %get-tuple-element.23), channel_id=1, source_target_pairs={{0,8},{2,10},{4,12},{6,14},{8,0},{10,2},{12,4},{14,6},{1,9},{3,11}... | collective-permute-start | bytes 294920 | tf_op jit(solution)/shard_map/ppermute | solution.py:330
  6.9 1.7 %collective-permute-start.6 = (bf16[320,128]{1,0:T(8,128)(2,1)S(1)}, bf16[320,128]{1,0:T(8,128)(2,1)S(1)}, u32[]{:S(2)}, u32[]{:S(2)}) collective-permute-start(bf16[320,128]{1,0:T(8,128)(2,1)S(1)} %get-tuple-element.24), channel_id=1, source_target_pairs={{0,2},{2,0},{4,6},{6,4},{8,10},{10,8},{12,14},{14,12},{1,3},{3,1},... | collective-permute-start | bytes 245768 | tf_op jit(solution)/shard_map/ppermute | solution.py:330
  8.5 1.4 %collective-permute-done.after_ref.refs_1_ = bf16[384,128]{1,0:T(8,128)(2,1)S(1)} collective-permute-done((bf16[384,128]{1,0:T(8,128)(2,1)S(1)}, bf16[384,128]{1,0:T(8,128)(2,1)S(1)}, u32[]{:S(2)}, u32[]{:S(2)}) %collective-permute-start) | collective-permute-done | bytes 98336 | tf_op jit(solution)/shard_map/ppermute | solution.py:330
  9.9 1.7 %collective-permute-start.1 = (bf16[320,128]{1,0:T(8,128)(2,1)S(1)}, bf16[320,128]{1,0:T(8,128)(2,1)S(1)}, u32[]{:S(2)}, u32[]{:S(2)}) collective-permute-start(bf16[320,128]{1,0:T(8,128)(2,1)S(1)} %slice.80), channel_id=1, source_target_pairs={{0,2},{2,0},{4,6},{6,4},{8,10},{10,8},{12,14},{14,12},{1,3},{3,1},... | collective-permute-start | bytes 245768 | tf_op jit(solution)/shard_map/ppermute | solution.py:330
  11.6 0.6 %collective-permute-done.2.refs_3_ = bf16[384,128]{1,0:T(8,128)(2,1)S(1)} collective-permute-done((bf16[384,128]{1,0:T(8,128)(2,1)S(1)}, bf16[384,128]{1,0:T(8,128)(2,1)S(1)}, u32[]{:S(2)}, u32[]{:S(2)}) %collective-permute-start.2) | collective-permute-done | bytes 98336 | tf_op jit(solution)/shard_map/ppermute | solution.py:330
  12.2 1.5 %collective-permute-start.3 = (bf16[320,128]{1,0:T(8,128)(2,1)S(1)}, bf16[320,128]{1,0:T(8,128)(2,1)S(1)}, u32[]{:S(2)}, u32[]{:S(2)}) collective-permute-start(bf16[320,128]{1,0:T(8,128)(2,1)S(1)} %slice.81), channel_id=1, source_target_pairs={{0,2},{2,0},{4,6},{6,4},{8,10},{10,8},{12,14},{14,12},{1,3},{3,1},... | collective-permute-start | bytes 245768 | tf_op jit(solution)/shard_map/ppermute | solution.py:330
  13.8 0.7 %collective-permute-done.4.refs_5_ = bf16[384,128]{1,0:T(8,128)(2,1)S(1)} collective-permute-done((bf16[384,128]{1,0:T(8,128)(2,1)S(1)}, bf16[384,128]{1,0:T(8,128)(2,1)S(1)}, u32[]{:S(2)}, u32[]{:S(2)}) %collective-permute-start.4) | collective-permute-done | bytes 98336 | tf_op jit(solution)/shard_map/ppermute | solution.py:330
  14.5 1.5 %collective-permute-start.5 = (bf16[320,128]{1,0:T(8,128)(2,1)S(1)}, bf16[320,128]{1,0:T(8,128)(2,1)S(1)}, u32[]{:S(2)}, u32[]{:S(2)}) collective-permute-start(bf16[320,128]{1,0:T(8,128)(2,1)S(1)} %slice.82), channel_id=1, source_target_pairs={{0,2},{2,0},{4,6},{6,4},{8,10},{10,8},{12,14},{14,12},{1,3},{3,1},... | collective-permute-start | bytes 245768 | tf_op jit(solution)/shard_map/ppermute | solution.py:330
  16.0 2.2 %shard_map.65.refs_8_ = bf16[4,32,128,128]{3,2,1,0:T(8,128)(2,1)S(1)} custom-call(bf16[384,128]{1,0:T(8,128)(2,1)S(1)} %collective-permute-done.after_ref.refs_1_, bf16[8,32,128,128]{3,2,1,0:T(8,128)(2,1)} %refs_9_.1), custom_call_target="tpu_custom_call" | custom-call | bytes 16777216 | tf_op jit(solution)/shard_map/pallas_call | solution.py:108
  18.3 0.7 %collective-permute-done.5.refs_4_ = bf16[320,128]{1,0:T(8,128)(2,1)S(1)} collective-permute-done((bf16[320,128]{1,0:T(8,128)(2,1)S(1)}, bf16[320,128]{1,0:T(8,128)(2,1)S(1)}, u32[]{:S(2)}, u32[]{:S(2)}) %collective-permute-start.5) | collective-permute-done | bytes 81952 | tf_op jit(solution)/shard_map/ppermute | solution.py:330
  18.9 5.1 %shard_map.66 = (bf16[288,128]{1,0:T(8,128)(2,1)S(1)}, bf16[288,128]{1,0:T(8,128)(2,1)S(1)}, bf16[288,128]{1,0:T(8,128)(2,1)S(1)}, bf16[288,128]{1,0:T(8,128)(2,...) custom-call(s32[8,32]{1,0:T(8,128)S(1)} %get-tuple-element.20.table_ref, ...), custom_call_target="tpu_custom_call" | custom-call | flops 536870912 | bytes 8388608 | tf_op jit(solution)/shard_map/pallas_call | solution.py:237
  24.0 1.7 %collective-permute-start.7 = (bf16[288,128]{1,0:T(8,128)(2,1)S(1)}, bf16[288,128]{1,0:T(8,128)(2,1)S(1)}, u32[]{:S(2)}, u32[]{:S(2)}) collective-permute-start(bf16[288,128]{1,0:T(8,128)(2,1)S(1)} %get-tuple-element.27), channel_id=1, source_target_pairs={{0,2},{2,0},{4,6},{6,4},{8,10},{10,8},{12,14},{14,12},{1,3},{3,1},... | collective-permute-start | bytes 221192 | tf_op jit(solution)/shard_map/ppermute | solution.py:330
  25.7 0.4 %collective-permute-start.9 = (bf16[288,128]{1,0:T(8,128)(2,1)S(1)}, bf16[288,128]{1,0:T(8,128)(2,1)S(1)}, u32[]{:S(2)}, u32[]{:S(2)}) collective-permute-start(bf16[288,128]{1,0:T(8,128)(2,1)S(1)} %get-tuple-element.29), channel_id=1, source_target_pairs={{0,2},{2,0},{4,6},{6,4},{8,10},{10,8},{12,14},{14,12},{1,3},{3,1},... | collective-permute-start | bytes 221192 | tf_op jit(solution)/shard_map/ppermute | solution.py:330
  26.1 1.2 %collective-permute-start.11 = (bf16[576,128]{1,0:T(8,128)(2,1)S(1)}, bf16[576,128]{1,0:T(8,128)(2,1)S(1)}, u32[]{:S(2)}, u32[]{:S(2)}) collective-permute-start(bf16[576,128]{1,0:T(8,128)(2,1)S(1)} %get-tuple-element.31), channel_id=1, source_target_pairs={{0,4},{2,6},{4,0},{6,2},{8,12},{10,14},{12,8},{14,10},{1,5},{3,7},... | collective-permute-start | bytes 442376 | tf_op jit(solution)/shard_map/ppermute | solution.py:330
  27.3 1.1 %collective-permute-done.7 = bf16[288,128]{1,0:T(8,128)(2,1)S(1)} collective-permute-done((bf16[288,128]{1,0:T(8,128)(2,1)S(1)}, bf16[288,128]{1,0:T(8,128)(2,1)S(1)}, u32[]{:S(2)}, u32[]{:S(2)}) %collective-permute-start.7) | collective-permute-done | bytes 73760 | tf_op jit(solution)/shard_map/ppermute | solution.py:330
  28.5 1.6 %collective-permute-start.8 = (bf16[320,128]{1,0:T(8,128)(2,1)S(1)}, bf16[320,128]{1,0:T(8,128)(2,1)S(1)}, u32[]{:S(2)}, u32[]{:S(2)}) collective-permute-start(bf16[320,128]{1,0:T(8,128)(2,1)S(1)} %pad_maximum_fusion), channel_id=1, source_target_pairs={{0,8},{2,10},{4,12},{6,14},{8,0},{10,2},{12,4},{14,6},{1,9},{3,11}... | collective-permute-start | bytes 245768 | tf_op jit(solution)/shard_map/ppermute | solution.py:330
  30.2 2.5 %collective-permute-start.10 = (bf16[320,128]{1,0:T(8,128)(2,1)S(1)}, bf16[320,128]{1,0:T(8,128)(2,1)S(1)}, u32[]{:S(2)}, u32[]{:S(2)}) collective-permute-start(bf16[320,128]{1,0:T(8,128)(2,1)S(1)} %pad_maximum_fusion.1), channel_id=1, source_target_pairs={{0,12},{2,14},{4,8},{6,10},{8,4},{10,6},{12,0},{14,2},{1,13},{3,15... | collective-permute-start | bytes 245768 | tf_op jit(solution)/shard_map/ppermute | solution.py:330
  32.9 1.1 %collective-permute-start.12 = (bf16[320,128]{1,0:T(8,128)(2,1)S(1)}, bf16[320,128]{1,0:T(8,128)(2,1)S(1)}, u32[]{:S(2)}, u32[]{:S(2)}) collective-permute-start(bf16[320,128]{1,0:T(8,128)(2,1)S(1)} %pad_maximum_fusion.2), channel_id=1, source_target_pairs={{0,2},{2,0},{4,6},{6,4},{8,10},{10,8},{12,14},{14,12},{1,3},{3,1},... | collective-permute-start | bytes 245768 | tf_op jit(solution)/shard_map/ppermute | solution.py:330
  33.9 1.4 %collective-permute-done.8.refs_0_ = bf16[320,128]{1,0:T(8,128)(2,1)S(1)} collective-permute-done((bf16[320,128]{1,0:T(8,128)(2,1)S(1)}, bf16[320,128]{1,0:T(8,128)(2,1)S(1)}, u32[]{:S(2)}, u32[]{:S(2)}) %collective-permute-start.8) | collective-permute-done | bytes 81952 | tf_op jit(solution)/shard_map/ppermute | solution.py:330
  35.4 1.3 %collective-permute-done.10.refs_1_ = bf16[320,128]{1,0:T(8,128)(2,1)S(1)} collective-permute-done((bf16[320,128]{1,0:T(8,128)(2,1)S(1)}, bf16[320,128]{1,0:T(8,128)(2,1)S(1)}, u32[]{:S(2)}, u32[]{:S(2)}) %collective-permute-start.10) | collective-permute-done | bytes 81952 | tf_op jit(solution)/shard_map/ppermute | solution.py:330
  36.7 0.7 %collective-permute-done.12.refs_2_ = bf16[320,128]{1,0:T(8,128)(2,1)S(1)} collective-permute-done((bf16[320,128]{1,0:T(8,128)(2,1)S(1)}, bf16[320,128]{1,0:T(8,128)(2,1)S(1)}, u32[]{:S(2)}, u32[]{:S(2)}) %collective-permute-start.12) | collective-permute-done | bytes 81952 | tf_op jit(solution)/shard_map/ppermute | solution.py:330
  37.4 0.8 %shard_map.67 = f32[4,8192]{1,0:T(4,128)} custom-call(f32[256,128]{1,0:T(8,128)S(1)} %get-tuple-element.19.scale_ref, bf16[320,128]{1,0:T(8,128)(2,1)S(1)} %collective-permute-done.8.refs_0_, bf16[320,128]{1,0:T(8,128)(2,1)S(1)} %collective-permute-done.10.refs_1_, bf16[320,128]{1,0:T(8,128)(2,1)S(1)} %collective-permute-done.12.refs_2_, ...), custom_call_target="tpu_custom_call" | custom-call | tf_op jit(solution)/shard_map/pallas_call | solution.py:288
  (25 shorter events, 0.3 us)
Async XLA Ops:
  1.1 8.8 %collective-permute-start = (bf16[384,128]{1,0:T(8,128)(2,1)S(1)}, bf16[384,128]{1,0:T(8,128)(2,1)S(1)}, u32[]{:S(2)}, u32[]{:S(2)}) collective-permute-start(bf16[384,128]{1,0:T(8,128)(2,1)S(1)} %get-tuple-element.21), channel_id=1, source_target_pairs={{0,12},{2,14},{4,8},{6,10},{8,4},{10,6},{12,0},{14,2},{1,13},{3,15... | collective-permute-start | bytes 294920 | tf_op jit(solution)/shard_map/ppermute | solution.py:330
  6.2 6.0 %collective-permute-start.2 = (bf16[384,128]{1,0:T(8,128)(2,1)S(1)}, bf16[384,128]{1,0:T(8,128)(2,1)S(1)}, u32[]{:S(2)}, u32[]{:S(2)}) collective-permute-start(bf16[384,128]{1,0:T(8,128)(2,1)S(1)} %get-tuple-element.22), channel_id=1, source_target_pairs={{0,4},{2,6},{4,0},{6,2},{8,12},{10,14},{12,8},{14,10},{1,5},{3,7},... | collective-permute-start | bytes 294920 | tf_op jit(solution)/shard_map/ppermute | solution.py:330
  6.2 8.3 %collective-permute-start.4 = (bf16[384,128]{1,0:T(8,128)(2,1)S(1)}, bf16[384,128]{1,0:T(8,128)(2,1)S(1)}, u32[]{:S(2)}, u32[]{:S(2)}) collective-permute-start(bf16[384,128]{1,0:T(8,128)(2,1)S(1)} %get-tuple-element.23), channel_id=1, source_target_pairs={{0,8},{2,10},{4,12},{6,14},{8,0},{10,2},{12,4},{14,6},{1,9},{3,11}... | collective-permute-start | bytes 294920 | tf_op jit(solution)/shard_map/ppermute | solution.py:330
  6.9 11.4 %collective-permute-start.6 = (bf16[320,128]{1,0:T(8,128)(2,1)S(1)}, bf16[320,128]{1,0:T(8,128)(2,1)S(1)}, u32[]{:S(2)}, u32[]{:S(2)}) collective-permute-start(bf16[320,128]{1,0:T(8,128)(2,1)S(1)} %get-tuple-element.24), channel_id=1, source_target_pairs={{0,2},{2,0},{4,6},{6,4},{8,10},{10,8},{12,14},{14,12},{1,3},{3,1},... | collective-permute-start | bytes 245768 | tf_op jit(solution)/shard_map/ppermute | solution.py:330
  9.9 8.3 %collective-permute-start.1 = (bf16[320,128]{1,0:T(8,128)(2,1)S(1)}, bf16[320,128]{1,0:T(8,128)(2,1)S(1)}, u32[]{:S(2)}, u32[]{:S(2)}) collective-permute-start(bf16[320,128]{1,0:T(8,128)(2,1)S(1)} %slice.80), channel_id=1, source_target_pairs={{0,2},{2,0},{4,6},{6,4},{8,10},{10,8},{12,14},{14,12},{1,3},{3,1},... | collective-permute-start | bytes 245768 | tf_op jit(solution)/shard_map/ppermute | solution.py:330
  12.2 6.0 %collective-permute-start.3 = (bf16[320,128]{1,0:T(8,128)(2,1)S(1)}, bf16[320,128]{1,0:T(8,128)(2,1)S(1)}, u32[]{:S(2)}, u32[]{:S(2)}) collective-permute-start(bf16[320,128]{1,0:T(8,128)(2,1)S(1)} %slice.81), channel_id=1, source_target_pairs={{0,2},{2,0},{4,6},{6,4},{8,10},{10,8},{12,14},{14,12},{1,3},{3,1},... | collective-permute-start | bytes 245768 | tf_op jit(solution)/shard_map/ppermute | solution.py:330
  14.5 4.4 %collective-permute-start.5 = (bf16[320,128]{1,0:T(8,128)(2,1)S(1)}, bf16[320,128]{1,0:T(8,128)(2,1)S(1)}, u32[]{:S(2)}, u32[]{:S(2)}) collective-permute-start(bf16[320,128]{1,0:T(8,128)(2,1)S(1)} %slice.82), channel_id=1, source_target_pairs={{0,2},{2,0},{4,6},{6,4},{8,10},{10,8},{12,14},{14,12},{1,3},{3,1},... | collective-permute-start | bytes 245768 | tf_op jit(solution)/shard_map/ppermute | solution.py:330
  24.0 4.4 %collective-permute-start.7 = (bf16[288,128]{1,0:T(8,128)(2,1)S(1)}, bf16[288,128]{1,0:T(8,128)(2,1)S(1)}, u32[]{:S(2)}, u32[]{:S(2)}) collective-permute-start(bf16[288,128]{1,0:T(8,128)(2,1)S(1)} %get-tuple-element.27), channel_id=1, source_target_pairs={{0,2},{2,0},{4,6},{6,4},{8,10},{10,8},{12,14},{14,12},{1,3},{3,1},... | collective-permute-start | bytes 221192 | tf_op jit(solution)/shard_map/ppermute | solution.py:330
  25.7 4.4 %collective-permute-start.9 = (bf16[288,128]{1,0:T(8,128)(2,1)S(1)}, bf16[288,128]{1,0:T(8,128)(2,1)S(1)}, u32[]{:S(2)}, u32[]{:S(2)}) collective-permute-start(bf16[288,128]{1,0:T(8,128)(2,1)S(1)} %get-tuple-element.29), channel_id=1, source_target_pairs={{0,2},{2,0},{4,6},{6,4},{8,10},{10,8},{12,14},{14,12},{1,3},{3,1},... | collective-permute-start | bytes 221192 | tf_op jit(solution)/shard_map/ppermute | solution.py:330
  26.1 6.6 %collective-permute-start.11 = (bf16[576,128]{1,0:T(8,128)(2,1)S(1)}, bf16[576,128]{1,0:T(8,128)(2,1)S(1)}, u32[]{:S(2)}, u32[]{:S(2)}) collective-permute-start(bf16[576,128]{1,0:T(8,128)(2,1)S(1)} %get-tuple-element.31), channel_id=1, source_target_pairs={{0,4},{2,6},{4,0},{6,2},{8,12},{10,14},{12,8},{14,10},{1,5},{3,7},... | collective-permute-start | bytes 442376 | tf_op jit(solution)/shard_map/ppermute | solution.py:330
  28.5 6.8 %collective-permute-start.8 = (bf16[320,128]{1,0:T(8,128)(2,1)S(1)}, bf16[320,128]{1,0:T(8,128)(2,1)S(1)}, u32[]{:S(2)}, u32[]{:S(2)}) collective-permute-start(bf16[320,128]{1,0:T(8,128)(2,1)S(1)} %pad_maximum_fusion), channel_id=1, source_target_pairs={{0,8},{2,10},{4,12},{6,14},{8,0},{10,2},{12,4},{14,6},{1,9},{3,11}... | collective-permute-start | bytes 245768 | tf_op jit(solution)/shard_map/ppermute | solution.py:330
  30.2 6.4 %collective-permute-start.10 = (bf16[320,128]{1,0:T(8,128)(2,1)S(1)}, bf16[320,128]{1,0:T(8,128)(2,1)S(1)}, u32[]{:S(2)}, u32[]{:S(2)}) collective-permute-start(bf16[320,128]{1,0:T(8,128)(2,1)S(1)} %pad_maximum_fusion.1), channel_id=1, source_target_pairs={{0,12},{2,14},{4,8},{6,10},{8,4},{10,6},{12,0},{14,2},{1,13},{3,15... | collective-permute-start | bytes 245768 | tf_op jit(solution)/shard_map/ppermute | solution.py:330
  32.9 4.5 %collective-permute-start.12 = (bf16[320,128]{1,0:T(8,128)(2,1)S(1)}, bf16[320,128]{1,0:T(8,128)(2,1)S(1)}, u32[]{:S(2)}, u32[]{:S(2)}) collective-permute-start(bf16[320,128]{1,0:T(8,128)(2,1)S(1)} %pad_maximum_fusion.2), channel_id=1, source_target_pairs={{0,2},{2,0},{4,6},{6,4},{8,10},{10,8},{12,14},{14,12},{1,3},{3,1},... | collective-permute-start | bytes 245768 | tf_op jit(solution)/shard_map/ppermute | solution.py:330
